TPU v7x, 128 devices: a whole 4x4x4 slice. The times are simulated.
128 devices in a mesh: seq: 16 (over x, y_hi, core), head: 8 (over z, y_lo).
Axes of the slice: x: 4, y: 4 (y_hi: 2, y_lo: 2; y = y_hi * 2 + y_lo), z: 4, core: 2. Of those that a mesh axis runs over, the one named last changes fastest.
Arguments:
- queries: bfloat16 [8192, 4096], P('seq', 'head'), may hold values from -15 to 15
- keys: bfloat16 [8192, 2048], P('seq', 'head'), may hold values from -6 to 6
- values: bfloat16 [8192, 2048], P('seq', 'head'), may hold values from -6 to 6
- out_grad: bfloat16 [8192, 4096], P('seq', 'head'), may hold values from -48 to 48
- normed: bfloat16 [8192, 4608], P('seq'), may hold values from -1.1953125 to 1.1953125
- w_query: bfloat16 [4608, 4096], P(None, 'head'), may hold values from -0.125 to 0.125
- w_key: bfloat16 [4608, 2048], P(None, 'head'), may hold values from -0.125 to 0.125
- w_value: bfloat16 [4608, 2048], P(None, 'head'), may hold values from -0.125 to 0.125
- valid_len: int32 [16], replicated, may hold values from 128 to 512, as said below
Outputs:
- grad_x: bfloat16 [8192, 4608], P('seq', 'head')
- grad_wq: bfloat16 [4608, 4096], P('seq', 'head')
- grad_wk: bfloat16 [4608, 2048], P('seq', 'head')
- grad_wv: bfloat16 [4608, 2048], P('seq', 'head')
Inputs may be any that keep to these rules, and one draw needn't show every extreme that they name: `valid_len`: every entry lies between 128 and 512; some shard is full and some shard has exactly 128 live slots.
All inputs are finite; a program needn't handle non-finite values.
Results may differ from a plain program's by a relative error of at most 0.024.
Values may be sent and summed in bfloat16 or wider, within the bound.
A program may use at most 192 MiB of HBM per device.

v0:
```python
import jax
import jax.numpy as jnp
from jax import lax
from jax.sharding import PartitionSpec as P

D = 4608
H = 32
HD = 128
WINDOW = 4096


SOFT_CAP = 50.0
ROPE_BASE = 10000.0


def passed_along(value, axis, by):
    size = lax.axis_size(axis)
    pairs = [(i, i + by) for i in range(size) if 0 <= i + by < size]
    return lax.ppermute(value, axis, pairs)


def rotate_back(gradient, positions, head_count):
    row_count = gradient.shape[0]
    half_width = HD // 2
    inverse_freq = ROPE_BASE ** (-(jnp.arange(half_width, dtype=jnp.float32) * (2.0 / HD)))
    angles = positions.astype(jnp.float32)[:, None] * inverse_freq[None, :]
    cosine = jnp.cos(angles)[:, None, :]
    sine_part = jnp.sin(angles)[:, None, :]
    per_head = gradient.reshape(row_count, head_count, HD)
    leading = per_head[:, :, :half_width]
    trailing = per_head[:, :, half_width:]
    rotated = jnp.concatenate(
        [leading * cosine + trailing * sine_part, trailing * cosine - leading * sine_part], axis=2
    )
    return rotated.reshape(row_count, head_count * HD)


def times_t(left, right):
    return lax.dot_general(
        left, right, (((1,), (1,)), ((), ())), preferred_element_type=jnp.float32
    )


def inner_rows(left, right):
    return lax.dot_general(
        left, right, (((0,), (0,)), ((), ())), preferred_element_type=jnp.float32
    )


def body(queries, keys, values, out_grad, normed, w_query, w_key, w_value, valid_len):
    row_count = queries.shape[0]
    kv_heads = keys.shape[1] // HD
    head_count = queries.shape[1] // HD
    group_size = head_count // kv_heads
    kv_width = kv_heads * HD
    hop_count = WINDOW // row_count
    score_scale = (D // H) ** (-0.5)
    shard_index = lax.axis_index("seq")
    last_shard = valid_len.shape[0] - 1
    row_iota = jnp.arange(row_count, dtype=jnp.int32)
    query_pos = shard_index * row_count + row_iota
    own_valid = row_iota < valid_len[shard_index]
    grad_rows = jnp.where(own_valid[:, None], out_grad, jnp.zeros_like(out_grad))
    query_blocks = queries.reshape(row_count, kv_heads, group_size, HD)
    grad_blocks = grad_rows.reshape(row_count, kv_heads, group_size, HD)
    key_value = jnp.concatenate([keys, values], axis=1)
    arrived = [key_value]
    moving = key_value
    for distance in range(1, hop_count + 1):
        moving = passed_along(moving, "seq", 1)
        arrived.append(moving)
    allowed_list = []
    capped_list = []
    running = jnp.zeros((kv_heads, group_size, row_count), jnp.float32)
    for distance in range(hop_count + 1):
        key_pos = (shard_index - distance) * row_count + row_iota
        owner = jnp.clip(shard_index - distance, 0, last_shard)
        key_valid = row_iota < valid_len[owner]
        offset_gap = query_pos[:, None] - key_pos[None, :]
        allowed = (
            (offset_gap >= 0)
            & (offset_gap < WINDOW)
            & (key_pos[None, :] >= 0)
            & (key_valid[None, :] | (offset_gap == 0))
        )
        key_block = arrived[distance][:, :kv_width].reshape(row_count, kv_heads, HD)
        raw_scores = (
            jnp.einsum(
                "qhgd,khd->hgqk", query_blocks, key_block, preferred_element_type=jnp.float32
            )
            * score_scale
        )
        capped = SOFT_CAP * jnp.tanh(raw_scores / SOFT_CAP)
        running = running + jnp.sum(jnp.where(allowed, jnp.exp(capped), 0.0), axis=-1)
        allowed_list.append(allowed)
        capped_list.append(capped)
    log_total = jnp.log(running)[..., None]
    attended = jnp.zeros((row_count, kv_heads, group_size, HD), jnp.float32)
    for distance in range(hop_count + 1):
        value_block = arrived[distance][:, kv_width:].reshape(row_count, kv_heads, HD)
        rounded = jnp.where(
            allowed_list[distance], jnp.exp(capped_list[distance] - log_total), 0.0
        ).astype(jnp.bfloat16)
        attended = attended + jnp.einsum(
            "hgqk,khd->qhgd", rounded, value_block, preferred_element_type=jnp.float32
        )
    row_delta = jnp.sum(grad_blocks.astype(jnp.float32) * attended, axis=-1)
    delta_cols = jnp.transpose(row_delta, (1, 2, 0))[..., None]
    query_grad = jnp.zeros((row_count, kv_heads, group_size, HD), jnp.float32)
    partials = [None] * (hop_count + 1)
    for distance in range(hop_count, -1, -1):
        key_block = arrived[distance][:, :kv_width].reshape(row_count, kv_heads, HD)
        value_block = arrived[distance][:, kv_width:].reshape(row_count, kv_heads, HD)
        capped = capped_list[distance]
        exact = jnp.where(allowed_list[distance], jnp.exp(capped - log_total), 0.0)
        rounded = exact.astype(jnp.bfloat16)
        grad_probs = jnp.einsum(
            "qhgd,khd->hgqk", grad_blocks, value_block, preferred_element_type=jnp.float32
        )
        grad_scores = (exact * (grad_probs - delta_cols) * (1.0 - (capped / SOFT_CAP) ** 2)).astype(
            jnp.bfloat16
        )
        query_grad = (
            query_grad
            + jnp.einsum(
                "hgqk,khd->qhgd", grad_scores, key_block, preferred_element_type=jnp.float32
            )
            * score_scale
        )
        key_grad = (
            jnp.einsum(
                "hgqk,qhgd->khd", grad_scores, query_blocks, preferred_element_type=jnp.float32
            )
            * score_scale
        )
        value_grad = jnp.einsum(
            "hgqk,qhgd->khd", rounded, grad_blocks, preferred_element_type=jnp.float32
        )
        partials[distance] = jnp.concatenate(
            [key_grad.reshape(row_count, kv_width), value_grad.reshape(row_count, kv_width)], axis=1
        )
    carried = partials[hop_count]
    for distance in range(hop_count - 1, -1, -1):
        carried = (
            passed_along(carried.astype(jnp.bfloat16), "seq", -1).astype(carried.dtype)
            + partials[distance]
        )
    query_pre = rotate_back(
        query_grad.reshape(row_count, head_count * HD), query_pos, head_count
    ).astype(jnp.bfloat16)
    key_pre = rotate_back(carried[:, :kv_width], query_pos, kv_heads).astype(jnp.bfloat16)
    value_pre = carried[:, kv_width:].astype(jnp.bfloat16)
    input_terms = (
        times_t(query_pre, w_query) + times_t(key_pre, w_key) + times_t(value_pre, w_value)
    )
    grad_x = lax.psum_scatter(
        input_terms.astype(jnp.bfloat16), "head", scatter_dimension=1, tiled=True
    )
    stacked = jnp.concatenate([query_pre, key_pre, value_pre], axis=1)
    weight_total = lax.psum_scatter(
        inner_rows(normed, stacked).astype(jnp.bfloat16), "seq", scatter_dimension=0, tiled=True
    ).astype(jnp.float32)
    query_cols = head_count * HD
    grad_wq = weight_total[:, :query_cols].astype(jnp.bfloat16)
    grad_wk = weight_total[:, query_cols : query_cols + kv_width].astype(jnp.bfloat16)
    grad_wv = weight_total[:, query_cols + kv_width :].astype(jnp.bfloat16)
    return (grad_x, grad_wq, grad_wk, grad_wv)


def solution(mesh):
    placed = (
        P("seq", "head"),
        P("seq", "head"),
        P("seq", "head"),
        P("seq", "head"),
        P("seq", None),
        P(None, "head"),
        P(None, "head"),
        P(None, "head"),
        P(),
    )
    return jax.shard_map(
        body,
        mesh=mesh,
        in_specs=placed,
        out_specs=(P("seq", "head"), P("seq", "head"), P("seq", "head"), P("seq", "head")),
        check_vma=False,
    )
```

profile of v0, /device:TPU:1, one launch (start us, length us, event | category | flops | bytes accessed | tf_op | source)
XLA Modules:
  0.0 520.9 jit_solution(3107178815283209028)
XLA Ops:
  10.4 6.2 %collective-permute-start = (bf16[512,512]{0,1:T(8,128)(2,1)}, bf16[512,512]{0,1:T(8,128)(2,1)}, u32[]{:S(2)}, u32[]{:S(2)}) collective-permute-start(bf16[512,512]{0,1:T(8,128)(2,1)} %pad_maximum_fusion), channel_id=1, source_target_pairs={{0,8},{8,16},{16,24},{24,32},{32,40},{40,48},{48,56},{56,64},{64,7... | collective-permute-start | bytes 1572872 | tf_op jit(solution)/shard_map/ppermute | solution.py:19
  17.8 1.7 reshape.361
  31.4 1.7 fusion.113
  33.1 2.5 fusion.48
  35.6 3.1 fusion.117
  38.7 1.9 collective-permute-start.1
  41.7 1.6 fusion.44
  43.3 3.8 collective-permute-done.1
  47.1 5.8 %collective-permute-start.2 = (bf16[512,512]{0,1:T(8,128)(2,1)S(1)}, bf16[512,512]{0,1:T(8,128)(2,1)S(1)}, u32[]{:S(2)}, u32[]{:S(2)}) collective-permute-start(bf16[512,512]{0,1:T(8,128)(2,1)S(1)} %collective-permute-done.1), channel_id=1, source_target_pairs={{0,8},{8,16},{16,24},{24,32},{32,40},{40,48},{48,56},{56,64},{64,7... | collective-permute-start | bytes 1572872 | tf_op jit(solution)/shard_map/ppermute | solution.py:19
  52.9 1.6 fusion.40
  54.5 4.5 collective-permute-done.2
  59.0 5.9 %collective-permute-start.3 = (bf16[512,512]{0,1:T(8,128)(2,1)S(1)}, bf16[512,512]{0,1:T(8,128)(2,1)S(1)}, u32[]{:S(2)}, u32[]{:S(2)}) collective-permute-start(bf16[512,512]{0,1:T(8,128)(2,1)S(1)} %collective-permute-done.2), channel_id=1, source_target_pairs={{0,8},{8,16},{16,24},{24,32},{32,40},{40,48},{48,56},{56,64},{64,7... | collective-permute-start | bytes 1572872 | tf_op jit(solution)/shard_map/ppermute | solution.py:19
  64.9 1.6 fusion.36
  66.5 4.5 collective-permute-done.3
  71.0 5.9 %collective-permute-start.4 = (bf16[512,512]{0,1:T(8,128)(2,1)S(1)}, bf16[512,512]{0,1:T(8,128)(2,1)S(1)}, u32[]{:S(2)}, u32[]{:S(2)}) collective-permute-start(bf16[512,512]{0,1:T(8,128)(2,1)S(1)} %collective-permute-done.3), channel_id=1, source_target_pairs={{0,8},{8,16},{16,24},{24,32},{32,40},{40,48},{48,56},{56,64},{64,7... | collective-permute-start | bytes 1572872 | tf_op jit(solution)/shard_map/ppermute | solution.py:19
  76.9 1.6 fusion.32
  78.5 4.5 collective-permute-done.4
  83.0 15.6 %collective-permute-start.5 = (bf16[512,512]{0,1:T(8,128)(2,1)S(1)}, bf16[512,512]{0,1:T(8,128)(2,1)S(1)}, u32[]{:S(2)}, u32[]{:S(2)}) collective-permute-start(bf16[512,512]{0,1:T(8,128)(2,1)S(1)} %collective-permute-done.4), channel_id=1, source_target_pairs={{0,8},{8,16},{16,24},{24,32},{32,40},{40,48},{48,56},{56,64},{64,7... | collective-permute-start | bytes 1572872 | tf_op jit(solution)/shard_map/ppermute | solution.py:19
  98.7 1.6 fusion.28
  100.3 2.0 collective-permute-start.6
  102.3 1.6 fusion.24
  103.9 4.5 collective-permute-done.6
  108.4 5.9 %collective-permute-start.7 = (bf16[512,512]{0,1:T(8,128)(2,1)S(1)}, bf16[512,512]{0,1:T(8,128)(2,1)S(1)}, u32[]{:S(2)}, u32[]{:S(2)}) collective-permute-start(bf16[512,512]{0,1:T(8,128)(2,1)S(1)} %collective-permute-done.6), channel_id=1, source_target_pairs={{0,8},{8,16},{16,24},{24,32},{32,40},{40,48},{48,56},{56,64},{64,7... | collective-permute-start | bytes 1572872 | tf_op jit(solution)/shard_map/ppermute | solution.py:19
  114.3 1.6 fusion.20
  115.9 4.5 collective-permute-done.7
  120.4 3.5 fusion.52
  125.4 3.6 fusion.93
  129.0 1.6 fusion.64
  130.6 1.6 fusion.65
  133.7 1.6 fusion.67
  138.5 1.8 fusion.70
  142.2 4.3 fusion.17
  146.5 2.2 fusion.15
  148.7 4.3 fusion.13
  153.0 2.2 fusion.11
  155.2 2.6 fusion.9
  157.8 2.2 fusion.7
  160.0 2.2 fusion.5
  162.1 2.2 fusion.3
  164.3 4.3 fusion.1
  172.0 2.1 collective-permute-start.8
  180.9 3.9 collective-permute-done.8
  184.9 1.9 collective-permute-start.9
  189.1 7.8 %collective-permute-done.9 = bf16[512,512]{0,1:T(8,128)(2,1)S(1)} collective-permute-done((bf16[512,512]{0,1:T(8,128)(2,1)S(1)}, bf16[512,512]{0,1:T(8,128)(2,1)S(1)}, u32[]{:S(2)}, u32[]{:S(2)}) %collective-permute-start.9) | collective-permute-done | bytes 524320 | tf_op jit(solution)/shard_map/ppermute | solution.py:19
  197.1 1.9 collective-permute-start.10
  201.3 7.8 %collective-permute-done.10 = bf16[512,512]{0,1:T(8,128)(2,1)S(1)} collective-permute-done((bf16[512,512]{0,1:T(8,128)(2,1)S(1)}, bf16[512,512]{0,1:T(8,128)(2,1)S(1)}, u32[]{:S(2)}, u32[]{:S(2)}) %collective-permute-start.10) | collective-permute-done | bytes 524320 | tf_op jit(solution)/shard_map/ppermute | solution.py:19
  209.3 1.9 collective-permute-start.11
  213.5 7.8 %collective-permute-done.11 = bf16[512,512]{0,1:T(8,128)(2,1)S(1)} collective-permute-done((bf16[512,512]{0,1:T(8,128)(2,1)S(1)}, bf16[512,512]{0,1:T(8,128)(2,1)S(1)}, u32[]{:S(2)}, u32[]{:S(2)}) %collective-permute-start.11) | collective-permute-done | bytes 524320 | tf_op jit(solution)/shard_map/ppermute | solution.py:19
  221.5 1.9 collective-permute-start.12
  225.6 7.9 %collective-permute-done.12 = bf16[512,512]{0,1:T(8,128)(2,1)S(1)} collective-permute-done((bf16[512,512]{0,1:T(8,128)(2,1)S(1)}, bf16[512,512]{0,1:T(8,128)(2,1)S(1)}, u32[]{:S(2)}, u32[]{:S(2)}) %collective-permute-start.12) | collective-permute-done | bytes 524320 | tf_op jit(solution)/shard_map/ppermute | solution.py:19
  233.7 2.1 collective-permute-start.13
  238.0 7.6 %collective-permute-done.13 = bf16[512,512]{0,1:T(8,128)(2,1)S(1)} collective-permute-done((bf16[512,512]{0,1:T(8,128)(2,1)S(1)}, bf16[512,512]{0,1:T(8,128)(2,1)S(1)}, u32[]{:S(2)}, u32[]{:S(2)}) %collective-permute-start.13) | collective-permute-done | bytes 524320 | tf_op jit(solution)/shard_map/ppermute | solution.py:19
  245.8 1.9 collective-permute-start.14
  249.4 8.5 %collective-permute-done.14 = bf16[512,512]{0,1:T(8,128)(2,1)S(1)} collective-permute-done((bf16[512,512]{0,1:T(8,128)(2,1)S(1)}, bf16[512,512]{0,1:T(8,128)(2,1)S(1)}, u32[]{:S(2)}, u32[]{:S(2)}) %collective-permute-start.14) | collective-permute-done | bytes 524320 | tf_op jit(solution)/shard_map/ppermute | solution.py:19
  258.0 1.9 collective-permute-start.15
  261.4 8.6 %collective-permute-done.15 = bf16[512,512]{0,1:T(8,128)(2,1)S(1)} collective-permute-done((bf16[512,512]{0,1:T(8,128)(2,1)S(1)}, bf16[512,512]{0,1:T(8,128)(2,1)S(1)}, u32[]{:S(2)}, u32[]{:S(2)}) %collective-permute-start.15) | collective-permute-done | bytes 524320 | tf_op jit(solution)/shard_map/ppermute | solution.py:19
  271.4 7.5 %fusion = bf16[4608,1024]{0,1:T(8,128)(2,1)} fusion(bf16[512,4608]{1,0:T(8,128)(2,1)S(1)} %bitcast.760, bf16[512,256]{0,1:T(8,128)(2,1)S(1)} %slice.154, bf16[512,256]{0,1:T(8,128)(2,1)S(1)} %bitcast.693, bf16[512,512]{0,1:T(8,128)(2,1)S(1)} %bitcast.682), kind=kOutput, calls=%fused_computation.2 | convolution fusion | flops 4839702528 | bytes 15204352 | tf_op jit(solution)/shard_map/dot_general | solution.py:45
  278.9 12.6 %copy.428 = bf16[4608,1024]{1,0:T(8,128)(2,1)} copy(bf16[4608,1024]{0,1:T(8,128)(2,1)} %fusion) | data formatting | bytes 18874368
  291.5 7.4 %fusion.192 = f32[512,4608]{0,1:T(8,128)} fusion(bf16[4608,512]{1,0:T(8,128)(2,1)} %param.14, bf16[512,512]{0,1:T(8,128)(2,1)S(1)} %bitcast.683), kind=kOutput, calls=%fused_computation.318 | convolution fusion | flops 2415919104 | bytes 14680064 | tf_op jit(solution)/shard_map/dot_general | solution.py:39
  300.9 7.7 %add_convert_fusion = bf16[512,4608]{0,1:T(8,128)(2,1)} fusion(f32[512,4608]{0,1:T(8,128)} %fusion.192, f32[512,4608]{0,1:T(8,128)S(1)} %fusion.193, bf16[4608,256]{1,0:T(8,128)(2,1)S(1)} %copy-done.3, f32[512,512]{0,1:T(8,128)S(1)} %copy-done.2), kind=kOutput, calls=%fused_computation.1 | convolution fusion | flops 1215037440 | bytes 26214400 | tf_op jit(solution)/shard_map/dot_general | solution.py:39
  308.6 101.1 %reduce-scatter.7.cloned.1.call-done = bf16[288,1024]{1,0:T(8,128)(2,1)} async-done(((bf16[4608,1024]{1,0:T(8,128)(2,1)}), bf16[288,1024]{1,0:T(8,128)(2,1)}) %reduce-scatter.7.cloned.1.call-update) | async-done | bytes 589840
  409.8 1.7 slice.142
  411.5 1.7 fusion.174
  413.2 100.6 %reduce-scatter.5.cloned.1.call-done = bf16[512,576]{0,1:T(8,128)(2,1)} async-done(((bf16[512,4608]{0,1:T(8,128)(2,1)}), bf16[512,576]{0,1:T(8,128)(2,1)}) %reduce-scatter.5.cloned.1.call-update) | async-done | bytes 589840 | tf_op jit(solution)/shard_map/reduce_scatter | solution.py:156
  (131 shorter events, 54.2 us)
Async XLA Ops:
  7.2 291.8 %copy-start = (bf16[4608,256]{1,0:T(8,128)(2,1)S(1)}, bf16[4608,256]{1,0:T(8,128)(2,1)}, u32[]{:S(2)}) copy-start(bf16[4608,256]{1,0:T(8,128)(2,1)} %param.15) | copy-start | bytes 7077892
  7.2 13.6 %copy-start.7 = (s32[16]{0:T(128)S(1)}, s32[16]{0:T(128)}, u32[]{:S(2)}) copy-start(s32[16]{0:T(128)} %param.17) | copy-start | bytes 196
  7.2 402.6 %reduce-scatter.7.cloned.1.call-start = ((), (), s32[]{:S(2)}) async-start(), calls=%async_computation.3 | async-start | bytes 10027008
  10.4 28.3 %collective-permute-start = (bf16[512,512]{0,1:T(8,128)(2,1)}, bf16[512,512]{0,1:T(8,128)(2,1)}, u32[]{:S(2)}, u32[]{:S(2)}) collective-permute-start(bf16[512,512]{0,1:T(8,128)(2,1)} %pad_maximum_fusion), channel_id=1, source_target_pairs={{0,8},{8,16},{16,24},{24,32},{32,40},{40,48},{48,56},{56,64},{64,7... | collective-permute-start | bytes 1572872 | tf_op jit(solution)/shard_map/ppermute | solution.py:19
  35.6 88.3 %copy-start.16 = (f32[2,512,512,2]{2,1,3,0:T(8,128)}, f32[2,512,512,2]{2,1,3,0:T(8,128)S(1)}, u32[]{:S(2)}) copy-start(f32[2,512,512,2]{2,1,3,0:T(8,128)S(1)} %get-tuple-element.74) | copy-start | bytes 12582916
  38.7 8.3 %collective-permute-start.1 = (bf16[512,512]{0,1:T(8,128)(2,1)}, bf16[512,512]{0,1:T(8,128)(2,1)S(1)}, u32[]{:S(2)}, u32[]{:S(2)}) collective-permute-start(bf16[512,512]{0,1:T(8,128)(2,1)} %collective-permute-done), channel_id=1, source_target_pairs={{0,8},{8,16},{16,24},{24,32},{32,40},{40,48},{48,56},{56,64},{64,7... | collective-permute-start | bytes 1572872 | tf_op jit(solution)/shard_map/ppermute | solution.py:19
  47.1 11.9 %collective-permute-start.2 = (bf16[512,512]{0,1:T(8,128)(2,1)S(1)}, bf16[512,512]{0,1:T(8,128)(2,1)S(1)}, u32[]{:S(2)}, u32[]{:S(2)}) collective-permute-start(bf16[512,512]{0,1:T(8,128)(2,1)S(1)} %collective-permute-done.1), channel_id=1, source_target_pairs={{0,8},{8,16},{16,24},{24,32},{32,40},{40,48},{48,56},{56,64},{64,7... | collective-permute-start | bytes 1572872 | tf_op jit(solution)/shard_map/ppermute | solution.py:19
  59.0 12.0 %collective-permute-start.3 = (bf16[512,512]{0,1:T(8,128)(2,1)S(1)}, bf16[512,512]{0,1:T(8,128)(2,1)S(1)}, u32[]{:S(2)}, u32[]{:S(2)}) collective-permute-start(bf16[512,512]{0,1:T(8,128)(2,1)S(1)} %collective-permute-done.2), channel_id=1, source_target_pairs={{0,8},{8,16},{16,24},{24,32},{32,40},{40,48},{48,56},{56,64},{64,7... | collective-permute-start | bytes 1572872 | tf_op jit(solution)/shard_map/ppermute | solution.py:19
  71.0 12.0 %collective-permute-start.4 = (bf16[512,512]{0,1:T(8,128)(2,1)S(1)}, bf16[512,512]{0,1:T(8,128)(2,1)S(1)}, u32[]{:S(2)}, u32[]{:S(2)}) collective-permute-start(bf16[512,512]{0,1:T(8,128)(2,1)S(1)} %collective-permute-done.3), channel_id=1, source_target_pairs={{0,8},{8,16},{16,24},{24,32},{32,40},{40,48},{48,56},{56,64},{64,7... | collective-permute-start | bytes 1572872 | tf_op jit(solution)/shard_map/ppermute | solution.py:19
  78.5 76.7 %copy-start.8 = (f32[2,512,512,2]{2,1,3,0:T(8,128)}, f32[2,512,512,2]{2,1,3,0:T(8,128)S(1)}, u32[]{:S(2)}) copy-start(f32[2,512,512,2]{2,1,3,0:T(8,128)S(1)} %get-tuple-element.68) | copy-start | bytes 12582916
  83.0 17.3 %collective-permute-start.5 = (bf16[512,512]{0,1:T(8,128)(2,1)S(1)}, bf16[512,512]{0,1:T(8,128)(2,1)S(1)}, u32[]{:S(2)}, u32[]{:S(2)}) collective-permute-start(bf16[512,512]{0,1:T(8,128)(2,1)S(1)} %collective-permute-done.4), channel_id=1, source_target_pairs={{0,8},{8,16},{16,24},{24,32},{32,40},{40,48},{48,56},{56,64},{64,7... | collective-permute-start | bytes 1572872 | tf_op jit(solution)/shard_map/ppermute | solution.py:19
  100.2 52.8 %copy-start.10 = (f32[2,512,512,2]{2,1,3,0:T(8,128)}, f32[2,512,512,2]{2,1,3,0:T(8,128)S(1)}, u32[]{:S(2)}) copy-start(f32[2,512,512,2]{2,1,3,0:T(8,128)S(1)} %get-tuple-element.66) | copy-start | bytes 12582916
  100.3 8.1 %collective-permute-start.6 = (bf16[512,512]{0,1:T(8,128)(2,1)S(1)}, bf16[512,512]{0,1:T(8,128)(2,1)S(1)}, u32[]{:S(2)}, u32[]{:S(2)}) collective-permute-start(bf16[512,512]{0,1:T(8,128)(2,1)S(1)} %collective-permute-done.5), channel_id=1, source_target_pairs={{0,8},{8,16},{16,24},{24,32},{32,40},{40,48},{48,56},{56,64},{64,7... | collective-permute-start | bytes 1572872 | tf_op jit(solution)/shard_map/ppermute | solution.py:19
  103.9 33.0 %copy-start.12 = (f32[2,512,512,2]{2,1,3,0:T(8,128)}, f32[2,512,512,2]{2,1,3,0:T(8,128)S(1)}, u32[]{:S(2)}) copy-start(f32[2,512,512,2]{2,1,3,0:T(8,128)S(1)} %get-tuple-element.64) | copy-start | bytes 12582916
  108.4 12.0 %collective-permute-start.7 = (bf16[512,512]{0,1:T(8,128)(2,1)S(1)}, bf16[512,512]{0,1:T(8,128)(2,1)S(1)}, u32[]{:S(2)}, u32[]{:S(2)}) collective-permute-start(bf16[512,512]{0,1:T(8,128)(2,1)S(1)} %collective-permute-done.6), channel_id=1, source_target_pairs={{0,8},{8,16},{16,24},{24,32},{32,40},{40,48},{48,56},{56,64},{64,7... | collective-permute-start | bytes 1572872 | tf_op jit(solution)/shard_map/ppermute | solution.py:19
  115.9 30.6 %copy-start.14 = (f32[2,512,512,2]{2,1,3,0:T(8,128)}, f32[2,512,512,2]{2,1,3,0:T(8,128)S(1)}, u32[]{:S(2)}) copy-start(f32[2,512,512,2]{2,1,3,0:T(8,128)S(1)} %get-tuple-element.62) | copy-start | bytes 12582916
  120.4 3.5 copy-start.6
  123.9 1.4 copy-start.5
  138.5 2.2 copy-start.18
  172.0 12.7 %collective-permute-start.8 = (bf16[512,512]{0,1:T(8,128)(2,1)S(1)}, bf16[512,512]{0,1:T(8,128)(2,1)S(1)}, u32[]{:S(2)}, u32[]{:S(2)}) collective-permute-start(bf16[512,512]{0,1:T(8,128)(2,1)S(1)} %pad_maximum_fusion.2), channel_id=1, source_target_pairs={{8,0},{16,8},{24,16},{32,24},{40,32},{48,40},{56,48},{64,56},{72,6... | collective-permute-start | bytes 1572872 | tf_op jit(solution)/shard_map/ppermute | solution.py:19
  176.4 1.0 copy-start.4
  177.3 2.2 copy-start.15
  180.9 6.8 %copy-start.13 = (f32[2,512,512,2]{2,1,3,0:T(8,128)S(1)}, f32[2,512,512,2]{2,1,3,0:T(8,128)}, u32[]{:S(2)}) copy-start(f32[2,512,512,2]{2,1,3,0:T(8,128)} %copy-done.12) | copy-start | bytes 12582916
  184.9 12.0 %collective-permute-start.9 = (bf16[512,512]{0,1:T(8,128)(2,1)S(1)}, bf16[512,512]{0,1:T(8,128)(2,1)S(1)}, u32[]{:S(2)}, u32[]{:S(2)}) collective-permute-start(bf16[512,512]{0,1:T(8,128)(2,1)S(1)} %fusion.95), channel_id=1, source_target_pairs={{8,0},{16,8},{24,16},{32,24},{40,32},{48,40},{56,48},{64,56},{72,6... | collective-permute-start | bytes 1572872 | tf_op jit(solution)/shard_map/ppermute | solution.py:19
  189.1 10.8 %copy-start.11 = (f32[2,512,512,2]{2,1,3,0:T(8,128)S(1)}, f32[2,512,512,2]{2,1,3,0:T(8,128)}, u32[]{:S(2)}) copy-start(f32[2,512,512,2]{2,1,3,0:T(8,128)} %copy-done.10) | copy-start | bytes 12582916
  197.1 12.0 %collective-permute-start.10 = (bf16[512,512]{0,1:T(8,128)(2,1)S(1)}, bf16[512,512]{0,1:T(8,128)(2,1)S(1)}, u32[]{:S(2)}, u32[]{:S(2)}) collective-permute-start(bf16[512,512]{0,1:T(8,128)(2,1)S(1)} %fusion.96), channel_id=1, source_target_pairs={{8,0},{16,8},{24,16},{32,24},{40,32},{48,40},{56,48},{64,56},{72,6... | collective-permute-start | bytes 1572872 | tf_op jit(solution)/shard_map/ppermute | solution.py:19
  201.3 10.8 %copy-start.9 = (f32[2,512,512,2]{2,1,3,0:T(8,128)S(1)}, f32[2,512,512,2]{2,1,3,0:T(8,128)}, u32[]{:S(2)}) copy-start(f32[2,512,512,2]{2,1,3,0:T(8,128)} %copy-done.8) | copy-start | bytes 12582916
  209.3 12.0 %collective-permute-start.11 = (bf16[512,512]{0,1:T(8,128)(2,1)S(1)}, bf16[512,512]{0,1:T(8,128)(2,1)S(1)}, u32[]{:S(2)}, u32[]{:S(2)}) collective-permute-start(bf16[512,512]{0,1:T(8,128)(2,1)S(1)} %fusion.97), channel_id=1, source_target_pairs={{8,0},{16,8},{24,16},{32,24},{40,32},{48,40},{56,48},{64,56},{72,6... | collective-permute-start | bytes 1572872 | tf_op jit(solution)/shard_map/ppermute | solution.py:19
  221.5 12.0 %collective-permute-start.12 = (bf16[512,512]{0,1:T(8,128)(2,1)S(1)}, bf16[512,512]{0,1:T(8,128)(2,1)S(1)}, u32[]{:S(2)}, u32[]{:S(2)}) collective-permute-start(bf16[512,512]{0,1:T(8,128)(2,1)S(1)} %fusion.98), channel_id=1, source_target_pairs={{8,0},{16,8},{24,16},{32,24},{40,32},{48,40},{56,48},{64,56},{72,6... | collective-permute-start | bytes 1572872 | tf_op jit(solution)/shard_map/ppermute | solution.py:19
  233.7 12.0 %collective-permute-start.13 = (bf16[512,512]{0,1:T(8,128)(2,1)S(1)}, bf16[512,512]{0,1:T(8,128)(2,1)S(1)}, u32[]{:S(2)}, u32[]{:S(2)}) collective-permute-start(bf16[512,512]{0,1:T(8,128)(2,1)S(1)} %fusion.99), channel_id=1, source_target_pairs={{8,0},{16,8},{24,16},{32,24},{40,32},{48,40},{56,48},{64,56},{72,6... | collective-permute-start | bytes 1572872 | tf_op jit(solution)/shard_map/ppermute | solution.py:19
  245.8 12.0 %collective-permute-start.14 = (bf16[512,512]{0,1:T(8,128)(2,1)S(1)}, bf16[512,512]{0,1:T(8,128)(2,1)S(1)}, u32[]{:S(2)}, u32[]{:S(2)}) collective-permute-start(bf16[512,512]{0,1:T(8,128)(2,1)S(1)} %fusion.100), channel_id=1, source_target_pairs={{8,0},{16,8},{24,16},{32,24},{40,32},{48,40},{56,48},{64,56},{72,6... | collective-permute-start | bytes 1572872 | tf_op jit(solution)/shard_map/ppermute | solution.py:19
  248.0 12.1 %copy-start.17 = (f32[2,512,512,2]{2,1,3,0:T(8,128)S(1)}, f32[2,512,512,2]{2,1,3,0:T(8,128)}, u32[]{:S(2)}) copy-start(f32[2,512,512,2]{2,1,3,0:T(8,128)} %copy-done.16) | copy-start | bytes 12582916
  258.0 12.0 %collective-permute-start.15 = (bf16[512,512]{0,1:T(8,128)(2,1)S(1)}, bf16[512,512]{0,1:T(8,128)(2,1)S(1)}, u32[]{:S(2)}, u32[]{:S(2)}) collective-permute-start(bf16[512,512]{0,1:T(8,128)(2,1)S(1)} %fusion.101), channel_id=1, source_target_pairs={{8,0},{16,8},{24,16},{32,24},{40,32},{48,40},{56,48},{64,56},{72,6... | collective-permute-start | bytes 1572872 | tf_op jit(solution)/shard_map/ppermute | solution.py:19
  260.0 11.4 %slice-start = ((s8[4718592]{0:T(1024)(128)(4,1)}), s8[4194304]{0:T(1024)(128)(4,1)S(1)}, s32[]{:S(2)}) async-start(s8[4718592]{0:T(1024)(128)(4,1)} %bitcast.759), calls=%async_computation.4 | async-start | bytes 8388608
  260.0 11.3 %slice-start.1 = ((s8[4718592]{0:T(1024)(128)(4,1)}), s8[524288]{0:T(1024)(128)(4,1)S(1)}, s32[]{:S(2)}) async-start(s8[4718592]{0:T(1024)(128)(4,1)} %bitcast.759), calls=%async_computation.5 | async-start | bytes 1048576
  270.2 1.0 copy-start.1
  291.5 222.3 %reduce-scatter.5.cloned.1.call-start = ((), (), s32[]{:S(2)}) async-start(), calls=%async_computation.2 | async-start | bytes 5308416 | tf_op jit(solution)/shard_map/reduce_scatter | solution.py:156
  299.0 1.4 copy-start.2
  299.0 2.0 copy-start.3
Sparse Core Ops, SparseCore 0:
  291.6 118.1 reduce-scatter.6
  412.8 101.0 reduce-scatter.4
where the time goes:
time: 531 us; the launch traced here: 521 us
  waiting for transfers between devices  288 us (54%)
  matrix products  108 us (20%)
  starting transfers between devices  65 us (12%)
  local copies, waits for them, and re-layouts  29.4 us (6%)
  other arithmetic  15.4 us (3%)
  between operations  15.4 us (3%)
    unnamed x3, waiting for transfers between devices  101 us
    reduce_scatter x1, waiting for transfers between devices, body(): lax.psum_scatter(input_terms.astype(jnp.bfloat16), 'head', scatter_dimens...  101 us
    ppermute x16, waiting for transfers between devices, passed_along(): return lax.ppermute(value, axis, pairs)  86 us
    ppermute x16, starting transfers between devices, passed_along(): return lax.ppermute(value, axis, pairs)  64.9 us
    dot_general x9, matrix products, body(): jnp.einsum('qhgd,khd->hgqk', grad_blocks, value_block, preferred_element_...  26.4 us
    unnamed x45, local copies, waits for them, and re-layouts  18 us
    dot_general x9, matrix products, body(): jnp.einsum('qhgd,khd->hgqk', query_blocks, key_block, preferred_element_t...  17.1 us
    dot_general x3, matrix products, times_t(): lax.dot_general(left, right, (((1,), (1,)), ((), ())), preferred_element_...  16.5 us
  transfers between devices with their start and end apart: 18, of which 16 were waited for; matrix products, arithmetic and copies ran while one was open for 14% of the time, Pallas kernels for 0%

commit v1 on v0

v1 whole, which is shorter than its diff:
```python
import functools

import jax
import jax.numpy as jnp
from jax import lax
from jax.experimental import pallas as pl
from jax.experimental.pallas import tpu as pltpu
from jax.sharding import PartitionSpec as P

D = 4608
H = 32
HD = 128
WINDOW = 4096
SOFT_CAP = 50.0
ROPE_BASE = 10000.0
SCALE = (D // H) ** (-0.5)

TOK = 512
NB = 10
TILE = 256
CHUNK = D // 4
HALF = CHUNK // 2
QTR = HALF // 2

BF = jnp.bfloat16
F32 = jnp.float32
MESH = pl.DeviceIdType.MESH
LOG2E = 1.4426950408889634


def nt(left, right):
    return lax.dot_general(left, right, (((1,), (1,)), ((), ())), preferred_element_type=F32)


def nn(left, right):
    return lax.dot_general(left, right, (((1,), (0,)), ((), ())), preferred_element_type=F32)


def here():
    s, h = lax.axis_index("seq"), lax.axis_index("head")
    return s // 4, (s // 2) % 2, s % 2, h // 2, h % 2


def at_seq(x, yh, core):
    return {"seq": (lax.rem(x + 4, 4) * 2 + yh) * 2 + core, "head": lax.axis_index("head")}


def at_head(z, yl):
    return {"seq": lax.axis_index("seq"), "head": lax.rem(z + 4, 4) * 2 + yl}


def remote(src, dst, send, recv, device):
    return pltpu.make_async_remote_copy(
        src_ref=src, dst_ref=dst, send_sem=send, recv_sem=recv, device_id=device, device_id_type=MESH
    )


def greet(devices):
    barrier = pltpu.get_barrier_semaphore()
    for device in devices:
        pl.semaphore_signal(barrier, inc=1, device_id=device, device_id_type=MESH)
    pl.semaphore_wait(barrier, len(devices))


def gather_kernel(
    q, g, k, v, n_ref, qx, gx, kv, nt_out, turned,
    loc_sem, swap_send, swap_recv, x_send, x_recv, y_send, y_recv, n_sem, n_send, n_recv,
):
    x, yh, core, _, _ = here()
    other = 1 - core
    partner = at_seq(x, yh, other)
    across = at_seq(x, 1 - yh, core)
    greet(
        [partner, across]
        + [at_seq(x + step, yh, c) for step in (1, -1, 2) for c in range(2)]
    )

    def head_cols(ref, head, width):
        return ref.at[:, pl.ds(pl.multiple_of(head * width, width), width)]

    local = [
        pltpu.make_async_copy(head_cols(k, core, HD), kv.at[8 + core, 0], loc_sem.at[0]),
        pltpu.make_async_copy(head_cols(v, core, HD), kv.at[8 + core, 1], loc_sem.at[1]),
        pltpu.make_async_copy(head_cols(q, core, 2 * HD), qx.at[core], loc_sem.at[2]),
        pltpu.make_async_copy(head_cols(g, core, 2 * HD), gx.at[core], loc_sem.at[3]),
    ]
    pairs = [
        (head_cols(k, other, HD), kv.at[8 + core, 0]),
        (head_cols(v, other, HD), kv.at[8 + core, 1]),
        (head_cols(q, other, 2 * HD), qx.at[core]),
        (head_cols(g, other, 2 * HD), gx.at[core]),
    ]
    swaps = [
        remote(src, dst, swap_send.at[i], swap_recv.at[i], partner)
        for i, (src, dst) in enumerate(pairs)
    ]
    for copy in local + swaps:
        copy.start()
    along = []
    for step in (1, 2):
        hops = []
        for kind, ref in enumerate((k, v)):
            for head in range(2):
                hops.append(
                    remote(
                        ref.at[:, head * HD : (head + 1) * HD],
                        kv.at[8 - 4 * step + core, kind],
                        x_send.at[step - 1, kind, head],
                        x_recv.at[step - 1, kind, core],
                        at_seq(x + step, yh, head),
                    )
                )
        along.append(hops)
        for copy in hops:
            copy.start()

    def arrived(step):
        for kind in range(2):
            for c in range(2):
                dst = kv.at[8 - 4 * step + c, kind]
                remote(dst, dst, x_send.at[step - 1, kind, c], x_recv.at[step - 1, kind, c], partner).wait_recv()

    def turn(i, carry):
        cols = pl.ds(pl.multiple_of(i * HD, HD), HD)
        turned[cols, :] = n_ref[:, cols].T
        return carry

    first_src = jnp.where(yh == 0, 8, 4)
    second_src = jnp.where(yh == 0, 4, 0)
    first = remote(kv.at[pl.ds(first_src, 2)], kv.at[pl.ds(6, 2)], y_send.at[0], y_recv.at[0], across)
    second = remote(kv.at[pl.ds(second_src, 2)], kv.at[pl.ds(2, 2)], y_send.at[1], y_recv.at[1], across)

    for copy in local:
        copy.wait()
    for copy in swaps:
        copy.wait_recv()

    @pl.when(yh == 0)
    def _():
        first.start()

    lax.fori_loop(0, D // HD, turn, 0)
    n_local = pltpu.make_async_copy(turned, nt_out.at[core], n_sem)
    n_swap = remote(turned, nt_out.at[core], n_send, n_recv, partner)
    n_local.start()
    n_swap.start()
    arrived(1)

    @pl.when(yh == 0)
    def _():
        second.start()

    @pl.when(yh == 1)
    def _():
        first.start()

    arrived(2)

    @pl.when(yh == 1)
    def _():
        second.start()

    n_local.wait()
    n_swap.wait()
    first.wait()
    second.wait()
    for copy in swaps + along[0] + along[1]:
        copy.wait_send()


def gather(queries, keys, values, grads, normed):
    any_space = pl.BlockSpec(memory_space=pl.ANY)
    dma = pltpu.SemaphoreType.DMA
    return pl.pallas_call(
        gather_kernel,
        out_shape=(
            jax.ShapeDtypeStruct((2, TOK, 2 * HD), BF),
            jax.ShapeDtypeStruct((2, TOK, 2 * HD), BF),
            jax.ShapeDtypeStruct((NB, 2, TOK, HD), BF),
            jax.ShapeDtypeStruct((2, D, TOK), BF),
        ),
        in_specs=[any_space] * 4 + [pl.BlockSpec(memory_space=pltpu.VMEM)],
        out_specs=(any_space,) * 4,
        scratch_shapes=[
            pltpu.VMEM((D, TOK), BF),
            dma((4,)), dma((4,)), dma((4,)), dma((2, 2, 2)), dma((2, 2, 2)),
            dma((2,)), dma((2,)), dma, dma, dma,
        ],
        compiler_params=pltpu.CompilerParams(
            collective_id=0, has_side_effects=True, vmem_limit_bytes=40 << 20
        ),
        name="gather",
    )(queries, grads, keys, values, normed)


def attend_kernel(
    valid, base, q, g, kv, cos, sin, dq_out, dkv_out, own_out,
    e_s, w_s, kt_s, vt_s, o_acc, dq_acc, dk_acc, dv_acc,
):
    first_shard = base[0]
    dk_acc[...] = jnp.zeros_like(dk_acc)
    dv_acc[...] = jnp.zeros_like(dv_acc)
    vt_s[:, HD:, :] = jnp.ones((2 * NB, 16, TILE), BF)

    def turn(b, carry):
        for kt in range(2):
            rows = slice(kt * TILE, (kt + 1) * TILE)
            kt_s[2 * b + kt] = kv[b, 0, rows, :].T
            vt_s[2 * b + kt, :HD, :] = kv[b, 1, rows, :].T
        return carry

    lax.fori_loop(0, NB, turn, 0)
    key_iota = lax.broadcasted_iota(jnp.int32, (TILE, 2 * TILE), 0)
    query_iota = lax.rem(lax.broadcasted_iota(jnp.int32, (TILE, 2 * TILE), 1), TILE)

    def query_tile(i, carry):
        r, qt = i // 2, lax.rem(i, 2)
        q_valid = valid[jnp.maximum(first_shard + 8 + r, 0)]
        q_rows = pl.ds(pl.multiple_of(qt * TILE, TILE), TILE)
        lanes = q_rows

        def info(t):
            j, kt = t // 2, lax.rem(t, 2)
            b = r + j
            shard = first_shard + b
            k_valid = valid[jnp.maximum(shard, 0)]
            active = (
                (shard >= 0)
                & (kt * TILE < k_valid)
                & jnp.logical_not((j == 8) & (kt > qt))
                & jnp.logical_not((j == 0) & (kt < qt))
            )
            edge = (((j == 8) | (j == 0)) & (kt == qt)) | ((kt + 1) * TILE > k_valid)
            return j, kt, b, k_valid, active, edge

        @pl.when(qt * TILE >= q_valid)
        def _():
            dq_out[r, :, lanes] = jnp.zeros((2 * HD, TILE), BF)

        @pl.when(qt * TILE < q_valid)
        def _():
            q_two = q[r, q_rows, :]
            g_two = g[r, q_rows, :]
            q_rows2 = jnp.concatenate([q_two[:, :HD], q_two[:, HD:]], axis=0)
            o_acc[...] = jnp.zeros_like(o_acc)

            def forward(t, carry):
                j, kt, b, k_valid, active, edge = info(t)
                rows = pl.ds(pl.multiple_of(kt * TILE, TILE), TILE)
                slot = pl.ds(pl.multiple_of(t * TILE, TILE), TILE)

                def tile(masked):
                    s = nt(kv[b, 0, rows, :], q_rows2)
                    th = jnp.tanh(s * (SCALE / SOFT_CAP))
                    e = jnp.exp2(th * (SOFT_CAP * LOG2E))
                    if masked:
                        gap = (query_iota + qt * TILE) - (key_iota + kt * TILE) + (8 - j) * TOK
                        allowed = (
                            (gap >= 0)
                            & (gap < WINDOW)
                            & ((key_iota + kt * TILE < k_valid) | (gap == 0))
                        )
                        e = jnp.where(allowed, e, 0.0)
                    eb = e.astype(BF)
                    e_s[slot, :] = eb
                    w_s[slot, :] = (e * (1.0 - th * th)).astype(BF)
                    o_acc[...] += nn(vt_s[2 * b + kt], eb)

                @pl.when(active & jnp.logical_not(edge))
                def _():
                    tile(False)

                @pl.when(active & edge)
                def _():
                    tile(True)

                return carry

            lax.fori_loop(0, 18, forward, 0)
            inv = 1.0 / o_acc[HD : HD + 1, :]
            g_rows2 = jnp.concatenate([g_two[:, :HD], g_two[:, HD:]], axis=0).astype(F32)
            live = query_iota[:1, :] + qt * TILE < q_valid
            g_t = jnp.where(live, g_rows2.T, 0.0) * inv
            delta = jnp.sum(g_t * o_acc[:HD, :], axis=0, keepdims=True) * inv
            gs_t = g_t.astype(BF)
            gs = g_t.T.astype(BF)
            dq_acc[...] = jnp.zeros_like(dq_acc)

            def backward(t, carry):
                j, kt, b, k_valid, active, edge = info(t)
                rows = pl.ds(pl.multiple_of(kt * TILE, TILE), TILE)
                slot = pl.ds(pl.multiple_of(t * TILE, TILE), TILE)

                @pl.when(active)
                def _():
                    dp = nn(kv[b, 1, rows, :], gs_t)
                    ds = (w_s[slot, :].astype(F32) * (dp - delta)).astype(BF)
                    dq_acc[...] += nn(kt_s[2 * b + kt], ds)
                    dk_acc[b, rows, :] += nn(ds, q_rows2)
                    dv_acc[b, rows, :] += nn(e_s[slot, :], gs)

                return carry

            lax.fori_loop(0, 18, backward, 0)
            dq = dq_acc[...] * SCALE
            c, s = cos[r, :, lanes], sin[r, :, lanes]
            for head in range(2):
                a = dq[: HD // 2, head * TILE : (head + 1) * TILE]
                z = dq[HD // 2 :, head * TILE : (head + 1) * TILE]
                dq_out[r, head * HD : head * HD + HD // 2, lanes] = (a * c + z * s).astype(BF)
                dq_out[r, head * HD + HD // 2 : (head + 1) * HD, lanes] = (z * c - a * s).astype(BF)

        return carry

    lax.fori_loop(0, 4, query_tile, 0)

    def give(b, carry):
        dkv_out[b, 0] = (dk_acc[b] * SCALE).astype(BF)
        dkv_out[b, 1] = dv_acc[b].astype(BF)
        return carry

    lax.fori_loop(0, 8, give, 0)
    for r in range(2):
        own_out[r, 0] = dk_acc[8 + r] * SCALE
        own_out[r, 1] = dv_acc[8 + r]


def attend(valid_len, base, qx, gx, kv, cos, sin):
    vmem = pl.BlockSpec(memory_space=pltpu.VMEM)
    smem = pl.BlockSpec(memory_space=pltpu.SMEM)
    return pl.pallas_call(
        attend_kernel,
        out_shape=(
            jax.ShapeDtypeStruct((2, 2 * HD, TOK), BF),
            jax.ShapeDtypeStruct((8, 2, TOK, HD), BF),
            jax.ShapeDtypeStruct((2, 2, TOK, HD), F32),
        ),
        in_specs=[smem, smem] + [vmem] * 5,
        out_specs=(vmem,) * 3,
        scratch_shapes=[
            pltpu.VMEM((18 * TILE, 2 * TILE), BF),
            pltpu.VMEM((18 * TILE, 2 * TILE), BF),
            pltpu.VMEM((2 * NB, HD, TILE), BF),
            pltpu.VMEM((2 * NB, HD + 16, TILE), BF),
            pltpu.VMEM((HD + 16, 2 * TILE), F32),
            pltpu.VMEM((HD, 2 * TILE), F32),
            pltpu.VMEM((NB, TOK, HD), F32),
            pltpu.VMEM((NB, TOK, HD), F32),
        ],
        compiler_params=pltpu.CompilerParams(vmem_limit_bytes=50 << 20),
        name="attend",
    )(valid_len, base, qx, gx, kv, cos, sin)


def finish_kernel(
    dq, dkv, own, turned_hbm, wq, wk, wv, cos, sin, gx_out, gq_out, gk_out, gv_out,
    n_buf, w_buf, t_buf, d_buf, y_buf, x_buf, near, far,
    xs, xr, zs, zr, xy, zy, half_buf, half_recv,
    load_sem, dq_sems, dk_sems, y_sems, x_sems, ring_send, ring_recv, pair_sems, core_sems,
):
    x, yh, core, z, yl = here()
    other = 1 - core
    partner = at_seq(x, yh, other)
    across = at_seq(x, 1 - yh, core)
    beside = at_head(z, 1 - yl)
    x_next, x_prev, x_far = at_seq(x + 1, yh, core), at_seq(x - 1, yh, core), at_seq(x + 2, yh, core)
    z_next, z_prev = at_head(z + 1, yl), at_head(z - 1, yl)
    greet([partner, across, beside, x_next, x_prev, x_far, z_next, z_prev])

    y_copies = [
        remote(dkv.at[pl.ds(6 - 4 * i, 2)], y_buf.at[i], y_sems.at[0, i], y_sems.at[1, i], across)
        for i in range(2)
    ]
    for copy in y_copies:
        copy.start()
    loads = [
        pltpu.make_async_copy(dkv.at[pl.ds(4, 2)], near, load_sem.at[0]),
        pltpu.make_async_copy(dkv.at[pl.ds(0, 2)], far, load_sem.at[1]),
        pltpu.make_async_copy(turned_hbm, n_buf, load_sem.at[2]),
        pltpu.make_async_copy(wq, w_buf.at[:, : 4 * HD], load_sem.at[3]),
        pltpu.make_async_copy(wk, w_buf.at[:, 4 * HD : 6 * HD], load_sem.at[4]),
        pltpu.make_async_copy(wv, w_buf.at[:, 6 * HD :], load_sem.at[5]),
    ]
    for copy in loads:
        copy.start()
    head_rows = pl.ds(pl.multiple_of(core * 2 * HD, 2 * HD), 2 * HD)
    dq_swap = remote(dq.at[other], d_buf.at[head_rows], dq_sems.at[0], dq_sems.at[1], partner)
    dq_swap.start()
    d_buf[head_rows, :] = dq[core]
    for r in range(2):
        t_buf[r, : 2 * HD, :] = dq[r]
    loads[0].wait()
    loads[1].wait()
    back_near = remote(near, x_buf.at[0], x_sems.at[0, 0], x_sems.at[1, 0], x_prev)
    back_far = remote(far, x_buf.at[1], x_sems.at[0, 1], x_sems.at[1, 1], x_far)

    def add_to(ref, index):
        ref[...] = (ref[...].astype(F32) + y_buf[index].astype(F32)).astype(BF)

    @pl.when(yh == 0)
    def _():
        back_far.start()

    y_copies[0].wait()

    @pl.when(yh == 1)
    def _():
        add_to(near, 0)
        back_near.start()

    y_copies[1].wait()

    @pl.when(yh == 0)
    def _():
        add_to(near, 1)
        back_near.start()

    @pl.when(yh == 1)
    def _():
        add_to(far, 1)
        back_far.start()

    keep = (yh == 0).astype(F32)
    back_near.wait()
    back_far.wait()
    for r in range(2):
        for kind in range(2):
            total = (
                own[r, kind]
                + y_buf[0, r, kind].astype(F32) * keep
                + x_buf[0, r, kind].astype(F32)
                + x_buf[1, r, kind].astype(F32)
            ).T
            if kind == 0:
                a, b = total[: HD // 2, :], total[HD // 2 :, :]
                c, s = cos[r], sin[r]
                total = jnp.concatenate([a * c + b * s, b * c - a * s], axis=0)
            t_buf[r, (2 + kind) * HD : (3 + kind) * HD, :] = total.astype(BF)
    dk_swaps = []
    for kind in range(2):
        rows = pl.ds(pl.multiple_of((4 + 2 * kind) * HD + core * HD, HD), HD)
        mine = pl.ds((2 + kind) * HD, HD)
        copy = remote(
            t_buf.at[other, mine], d_buf.at[rows], dk_sems.at[0, kind], dk_sems.at[1, kind], partner
        )
        copy.start()
        dk_swaps.append(copy)
        d_buf[rows, :] = t_buf[core, mine, :]

    for copy in loads[2:]:
        copy.wait()

    def weight_rows(place, half):
        rows = pl.ds(pl.multiple_of(place * CHUNK + half * HALF, QTR), HALF)
        return nt(n_buf[0, rows, :], t_buf[0]) + nt(n_buf[1, rows, :], t_buf[1])

    def input_rows(place, half):
        rows = pl.ds(pl.multiple_of(place * CHUNK + half * HALF, QTR), HALF)
        return nn(w_buf[rows, :], d_buf[...])

    send, recv = (xs, zs), (xr, zr)
    ahead, behind = (x_next, z_next), (x_prev, z_prev)
    place = (x, z)
    terms = (weight_rows, input_rows)

    def compute(axis, slot, step):
        where = lax.rem(place[axis] + step, 4)

        def one(half, carry):
            rows = pl.ds(pl.multiple_of(half * HALF, HALF), HALF)
            send[axis][slot, rows, :] = terms[axis](where, half).astype(BF)
            return carry

        lax.fori_loop(0, 2, one, 0)

    def halves(axis):
        top, low = pl.ds(0, HALF), pl.ds(HALF, HALF)
        return (
            remote(send[axis].at[0, top], recv[axis].at[0, top], ring_send.at[axis, 0], ring_recv.at[axis, 0], ahead[axis]),
            remote(send[axis].at[0, low], recv[axis].at[0, low], ring_send.at[axis, 1], ring_recv.at[axis, 1], behind[axis]),
        )

    def wholes(axis):
        return (
            remote(send[axis].at[1], recv[axis].at[1], ring_send.at[axis, 2], ring_recv.at[axis, 2], ahead[axis]),
            remote(send[axis].at[2], recv[axis].at[2], ring_send.at[axis, 3], ring_recv.at[axis, 3], behind[axis]),
        )

    half_copies = [None, None]
    whole_copies = [None, None]
    for axis in range(2):
        if axis == 1:
            dq_swap.wait()
            for copy in dk_swaps:
                copy.wait()
        compute(axis, 0, 2)
        half_copies[axis] = halves(axis)
        for copy in half_copies[axis]:
            copy.start()
    for axis in range(2):
        compute(axis, 1, 1)
        compute(axis, 2, 3)
    for axis in range(2):
        whole_copies[axis] = wholes(axis)
        half_copies[axis][0].wait()
        top = slice(0, HALF)
        send[axis][1, top, :] = (send[axis][1, top, :].astype(F32) + recv[axis][0, top, :].astype(F32)).astype(BF)
        whole_copies[axis][0].start()
        half_copies[axis][1].wait()
        low = slice(HALF, CHUNK)
        send[axis][2, low, :] = (send[axis][2, low, :].astype(F32) + recv[axis][0, low, :].astype(F32)).astype(BF)
        whole_copies[axis][1].start()
    side = (yh, yl)
    side_device = (across, beside)
    pair_buf = (xy, zy)
    for axis in range(2):
        compute(axis, 3, 0)
    pair_copies = []
    for axis in range(2):
        for copy in whole_copies[axis]:
            copy.wait()

        def summed(half):
            rows = pl.ds(pl.multiple_of(half * HALF, HALF), HALF)
            return (
                send[axis][3, rows, :].astype(F32)
                + recv[axis][1, rows, :].astype(F32)
                + recv[axis][2, rows, :].astype(F32)
            )

        pair_buf[axis][0] = summed(1 - side[axis]).astype(BF)
        copy = remote(pair_buf[axis].at[0], pair_buf[axis].at[1], pair_sems.at[0, axis], pair_sems.at[1, axis], side_device[axis])
        copy.start()
        pair_copies.append(copy)
        pair_buf[axis][2] = summed(side[axis]).astype(BF)
    pair_copies[0].wait()
    half_buf[...] = (xy[1].astype(F32) + xy[2].astype(F32)).astype(BF)
    my_rows = pl.ds(pl.multiple_of(core * QTR, QTR), QTR)
    its_rows = pl.ds(pl.multiple_of(other * QTR, QTR), QTR)
    last = remote(half_buf.at[its_rows], half_recv, core_sems.at[0], core_sems.at[1], partner)
    last.start()
    pair_copies[1].wait()
    gx_out[...] = (zy[1].astype(F32) + zy[2].astype(F32)).T.astype(BF)
    last.wait()
    for block, head in ((half_buf[my_rows, :], core), (half_recv[...], other)):
        gq_out[:, pl.ds(pl.multiple_of(head * 2 * HD, 2 * HD), 2 * HD)] = block[:, : 2 * HD]
        gk_out[:, pl.ds(pl.multiple_of(head * HD, HD), HD)] = block[:, 2 * HD : 3 * HD]
        gv_out[:, pl.ds(pl.multiple_of(head * HD, HD), HD)] = block[:, 3 * HD :]


def finish(dq, dkv, own, turned, wq, wk, wv, cos, sin):
    vmem = pl.BlockSpec(memory_space=pltpu.VMEM)
    any_space = pl.BlockSpec(memory_space=pl.ANY)
    dma = pltpu.SemaphoreType.DMA
    return pl.pallas_call(
        finish_kernel,
        out_shape=(
            jax.ShapeDtypeStruct((TOK, HALF), BF),
            jax.ShapeDtypeStruct((QTR, 4 * HD), BF),
            jax.ShapeDtypeStruct((QTR, 2 * HD), BF),
            jax.ShapeDtypeStruct((QTR, 2 * HD), BF),
        ),
        in_specs=[vmem, any_space, vmem, any_space, any_space, any_space, any_space, vmem, vmem],
        out_specs=(vmem,) * 4,
        scratch_shapes=[
            pltpu.VMEM((2, D, TOK), BF),
            pltpu.VMEM((D, 8 * HD), BF),
            pltpu.VMEM((2, 4 * HD, TOK), BF),
            pltpu.VMEM((8 * HD, TOK), BF),
            pltpu.VMEM((2, 2, 2, TOK, HD), BF),
            pltpu.VMEM((2, 2, 2, TOK, HD), BF),
            pltpu.VMEM((2, 2, TOK, HD), BF),
            pltpu.VMEM((2, 2, TOK, HD), BF),
            pltpu.VMEM((4, CHUNK, TOK), BF),
            pltpu.VMEM((3, CHUNK, TOK), BF),
            pltpu.VMEM((4, CHUNK, TOK), BF),
            pltpu.VMEM((3, CHUNK, TOK), BF),
            pltpu.VMEM((3, HALF, TOK), BF),
            pltpu.VMEM((3, HALF, TOK), BF),
            pltpu.VMEM((HALF, TOK), BF),
            pltpu.VMEM((QTR, TOK), BF),
            dma((6,)), dma((2,)), dma((2, 2)), dma((2, 2)), dma((2, 2)),
            dma((2, 4)), dma((2, 4)), dma((2, 2)), dma((2,)),
        ],
        compiler_params=pltpu.CompilerParams(
            collective_id=1, has_side_effects=True, vmem_limit_bytes=58 << 20
        ),
        name="finish",
    )(dq, dkv, own, turned, wq, wk, wv, cos, sin)


def body(queries, keys, values, out_grad, normed, w_query, w_key, w_value, valid_len):
    chip = lax.axis_index("seq") // 2
    inverse_freq = ROPE_BASE ** (-(jnp.arange(HD // 2, dtype=F32) * (2.0 / HD)))
    slots = (chip * 2 * TOK + jnp.arange(2 * TOK, dtype=jnp.int32)).astype(F32).reshape(2, 1, TOK)
    angles = slots * inverse_freq[None, :, None]
    cos, sin = jnp.cos(angles), jnp.sin(angles)
    base = (2 * chip - 8).astype(jnp.int32).reshape(1)
    qx, gx, kv, turned = gather(queries, keys, values, out_grad, normed)
    dq, dkv, own = attend(valid_len, base, qx, gx, kv, cos, sin)
    return finish(dq, dkv, own, turned, w_query, w_key, w_value, cos, sin)


def solution(mesh):
    both = P("seq", "head")
    placed = (both, both, both, both, P("seq", None), P(None, "head"), P(None, "head"), P(None, "head"), P())
    return jax.shard_map(
        body, mesh=mesh, in_specs=placed, out_specs=(both,) * 4, check_vma=False
    )
```

time: 531 us -> 244 us (0.46); the launches traced: 521 us -> 244 us
  waiting for transfers between devices: 288 us -> 0 us
  Pallas kernels: 0 us -> 225 us
  matrix products: 108 us -> 0 us
  starting transfers between devices: 65 us -> 0 us
  between operations: 15.4 us -> 0.72 us
  other arithmetic: 15.4 us -> 1 us
  local copies, waits for them, and re-layouts: 29.4 us -> 16.7 us
    pallas_call x0 -> x3, Pallas kernels: none -> 225 us  [the longest x1 167 us: finish(): pl.pallas_call(finish_kernel, out_shape=(jax.ShapeDtypeStruct((TOK, HALF)...]
    dot_general x58 -> x0, matrix products: 108 us -> none  [the longest x9 26.4 us: body(): jnp.einsum('qhgd,khd->hgqk', grad_blocks, value_block, preferred_element_...]
    unnamed x3 -> x0, waiting for transfers between devices: 101 us -> none
    reduce_scatter x1 -> x0, waiting for transfers between devices: 101 us -> none  [body(): lax.psum_scatter(input_terms.astype(jnp.bfloat16), 'head', scatter_dimens...]
    ppermute x16 -> x0, waiting for transfers between devices: 86 us -> none  [passed_along(): return lax.ppermute(value, axis, pairs)]
    ppermute x16 -> x0, starting transfers between devices: 64.9 us -> none  [passed_along(): return lax.ppermute(value, axis, pairs)]
    lt x6 -> x0, other arithmetic: 6.24 us -> none  [the longest x5 5.68 us: body(): key_valid = row_iota < valid_len[owner]]
    unnamed x45 -> x25, local copies, waits for them, and re-layouts: 18 us -> 14.6 us
  transfers between devices with their start and end apart: 18 -> 0, of which waited for: 16 -> 0; matrix products, arithmetic and copies ran while one was open for 14% -> 0% of each run, Pallas kernels for 0% -> 0%
where the time goes in v1:
time: 244 us
  Pallas kernels  225 us (92%)
  local copies, waits for them, and re-layouts  16.7 us (7%)
    pallas_call x1, Pallas kernels, finish(): pl.pallas_call(finish_kernel, out_shape=(jax.ShapeDtypeStruct((TOK, HALF)...  167 us
    pallas_call x1, Pallas kernels, gather(): pl.pallas_call(gather_kernel, out_shape=(jax.ShapeDtypeStruct((2, TOK, 2...  42.6 us
    pallas_call x1, Pallas kernels, attend(): pl.pallas_call(attend_kernel, out_shape=(jax.ShapeDtypeStruct((2, 2 * HD,...  15.5 us
    unnamed x25, local copies, waits for them, and re-layouts  14.6 us

profile of v1, /device:TPU:1, one launch (start us, length us, event | category | flops | bytes accessed | tf_op | source)
XLA Modules:
  0.0 243.7 jit_solution(10925323479001479163)
XLA Ops:
  0.7 1.0 multiply_sine_fusion
  1.7 0.0 copy-start.2
  1.7 0.0 copy-start.3
  1.7 0.0 copy-start
  1.7 2.5 %copy-done = bf16[512,4608]{1,0:T(8,128)(2,1)S(1)} copy-done((bf16[512,4608]{1,0:T(8,128)(2,1)S(1)}, bf16[512,4608]{1,0:T(8,128)(2,1)}, u32[]{:S(2)}) %copy-start) | copy-done | bytes 4718616
  4.2 0.0 copy-start.5
  4.2 1.0 copy-done.5
  5.3 0.0 copy-start.6
  5.3 1.0 copy-done.6
  6.3 0.0 copy-start.8
  6.3 0.9 copy-done.8
  7.2 0.0 copy-start.9
  7.2 0.9 copy-done.9
  8.2 0.0 copy-start.10
  8.2 42.6 %gather.1 = (bf16[2,512,256]{2,1,0:T(8,128)(2,1)S(1)}, bf16[2,512,256]{2,1,0:T(8,128)(2,1)S(1)}, bf16[10,2,512,128]{3,2,1,0:T(8,128)(2,1)S(1)}, bf16[2,4608,512]{2,1,0:T(8,128)(2,1)}) custom-call(bf16[512,512]{1,0:T(8,128)(2,1)S(1)} %copy-done.5, bf16[512,512]{1,0:T(8,128)(2,1)S(1)} %copy-done.6, bf16[512,256]{1,0:T(8,128)(2,1)S(1)} %copy-done.8, ...), custom_call_target="tpu_custom_call" | custom-call | tf_op jit(solution)/shard_map/gather/pallas_call | solution.py:174
  50.8 0.0 copy-start.1
  50.8 1.5 copy-done.1
  52.3 0.0 copy-done.2
  52.3 0.0 copy-done.3
  52.3 0.0 copy-done.10
  52.3 15.5 %attend.1 = (bf16[2,256,512]{2,1,0:T(8,128)(2,1)S(1)}, bf16[8,2,512,128]{3,2,1,0:T(8,128)(2,1)}, f32[2,2,512,128]{3,2,1,0:T(8,128)S(1)}) custom-call(s32[16]{0:T(128)S(1)} %copy-done.10, s32[1]{0:T(128)} %bitcast.base, bf16[2,512,256]{2,1,0:T(8,128)(2,1)S(1)} %get-tuple-element.11.q, bf16[2,512,256]{2,1,0:T(8,128)(2,1)S(1)} %get-tuple-element.12.g, ...), custom_call_target="tpu_custom_call" | custom-call | tf_op jit(solution)/shard_map/attend/pallas_call | solution.py:331
  67.7 0.0 copy-start.4
  67.7 1.0 copy-done.4
  68.7 0.0 copy-start.7
  68.7 0.8 copy-done.7
  69.5 167.2 %finish.1 = (bf16[512,576]{1,0:T(8,128)(2,1)}, bf16[288,512]{1,0:T(8,128)(2,1)}, bf16[288,256]{1,0:T(8,128)(2,1)}, bf16[288,256]{1,0:T(8,128)(2,1)}) custom-call(bf16[2,256,512]{2,1,0:T(8,128)(2,1)} %copy-done.7, bf16[8,2,512,128]{3,2,1,0:T(8,128)(2,1)} %get-tuple-element.15.dkv, f32[2,2,512,128]{3,2,1,0:T(8,128)} %copy-done.4, ...), custom_call_target="tpu_custom_call" | custom-call | tf_op jit(solution)/shard_map/finish/pallas_call | solution.py:555
  236.7 2.1 copy.13
  238.9 1.7 copy.17
  240.6 1.6 copy.18
  242.2 1.6 copy.19
  (2 shorter events, 0.0 us)
Async XLA Ops:
  1.7 50.6 %copy-start.2 = (f32[2,64,512]{2,1,0:T(8,128)}, f32[2,64,512]{2,1,0:T(8,128)S(1)}, u32[]{:S(2)}) copy-start(f32[2,64,512]{2,1,0:T(8,128)S(1)} %get-tuple-element.22.sin) | copy-start | bytes 786436
  1.7 50.6 %copy-start.3 = (f32[2,64,512]{2,1,0:T(8,128)}, f32[2,64,512]{2,1,0:T(8,128)S(1)}, u32[]{:S(2)}) copy-start(f32[2,64,512]{2,1,0:T(8,128)S(1)} %get-tuple-element.23.cos) | copy-start | bytes 786436
  1.7 2.5 %copy-start = (bf16[512,4608]{1,0:T(8,128)(2,1)S(1)}, bf16[512,4608]{1,0:T(8,128)(2,1)}, u32[]{:S(2)}) copy-start(bf16[512,4608]{1,0:T(8,128)(2,1)} %n_ref.1) | copy-start | bytes 14155780
  4.2 1.0 copy-start.5
  5.3 1.0 copy-start.6
  6.3 0.9 copy-start.8
  7.2 0.9 copy-start.9
  8.2 44.1 %copy-start.10 = (s32[16]{0:T(128)S(1)}, s32[16]{0:T(128)}, u32[]{:S(2)}) copy-start(s32[16]{0:T(128)} %valid.1) | copy-start | bytes 196
  50.8 1.5 copy-start.1
  67.7 1.0 copy-start.4
  68.7 0.8 copy-start.7

commit v2 on v1

v2 whole, which is shorter than its diff:
```python
import functools

import jax
import jax.numpy as jnp
from jax import lax
from jax.experimental import pallas as pl
from jax.experimental.pallas import tpu as pltpu
from jax.sharding import PartitionSpec as P

D = 4608
H = 32
HD = 128
WINDOW = 4096
SOFT_CAP = 50.0
ROPE_BASE = 10000.0
SCALE = (D // H) ** (-0.5)

TOK = 512
NB = 10
TILE = 256
CHUNK = D // 4
HALF = CHUNK // 2
QTR = HALF // 2

BF = jnp.bfloat16
F32 = jnp.float32
MESH = pl.DeviceIdType.MESH
LOG2E = 1.4426950408889634


def nt(left, right):
    return lax.dot_general(left, right, (((1,), (1,)), ((), ())), preferred_element_type=F32)


def nn(left, right):
    return lax.dot_general(left, right, (((1,), (0,)), ((), ())), preferred_element_type=F32)


def here():
    s, h = lax.axis_index("seq"), lax.axis_index("head")
    return s // 4, (s // 2) % 2, s % 2, h // 2, h % 2


def at_seq(x, yh, core):
    return {"seq": (lax.rem(x + 4, 4) * 2 + yh) * 2 + core, "head": lax.axis_index("head")}


def at_head(z, yl):
    return {"seq": lax.axis_index("seq"), "head": lax.rem(z + 4, 4) * 2 + yl}


def remote(src, dst, send, recv, device):
    return pltpu.make_async_remote_copy(
        src_ref=src, dst_ref=dst, send_sem=send, recv_sem=recv, device_id=device, device_id_type=MESH
    )


def greet(devices):
    barrier = pltpu.get_barrier_semaphore()
    for device in devices:
        pl.semaphore_signal(barrier, inc=1, device_id=device, device_id_type=MESH)
    pl.semaphore_wait(barrier, len(devices))


def gather_kernel(
    q, g, k, v, n_hbm, qx, gx, kv, nt_out, n_ref, turned,
    n_load_sem, loc_sem, swap_send, swap_recv, x_send, x_recv, y_send, y_recv, n_sem, n_send, n_recv,
):
    x, yh, core, _, _ = here()
    other = 1 - core
    partner = at_seq(x, yh, other)
    across = at_seq(x, 1 - yh, core)
    greet(
        [partner, across]
        + [at_seq(x + step, yh, c) for step in (1, -1, 2) for c in range(2)]
    )

    def head_cols(ref, head, width):
        return ref.at[:, pl.ds(pl.multiple_of(head * width, width), width)]

    local = [
        pltpu.make_async_copy(head_cols(k, core, HD), kv.at[8 + core, 0], loc_sem.at[0]),
        pltpu.make_async_copy(head_cols(v, core, HD), kv.at[8 + core, 1], loc_sem.at[1]),
        pltpu.make_async_copy(head_cols(q, core, 2 * HD), qx.at[core], loc_sem.at[2]),
        pltpu.make_async_copy(head_cols(g, core, 2 * HD), gx.at[core], loc_sem.at[3]),
    ]
    pairs = [
        (head_cols(k, other, HD), kv.at[8 + core, 0]),
        (head_cols(v, other, HD), kv.at[8 + core, 1]),
        (head_cols(q, other, 2 * HD), qx.at[core]),
        (head_cols(g, other, 2 * HD), gx.at[core]),
    ]
    swaps = [
        remote(src, dst, swap_send.at[i], swap_recv.at[i], partner)
        for i, (src, dst) in enumerate(pairs)
    ]
    for copy in local + swaps:
        copy.start()
    along = []
    for step in (1, 2):
        hops = []
        for kind, ref in enumerate((k, v)):
            for head in range(2):
                hops.append(
                    remote(
                        ref.at[:, head * HD : (head + 1) * HD],
                        kv.at[8 - 4 * step + core, kind],
                        x_send.at[step - 1, kind, head],
                        x_recv.at[step - 1, kind, core],
                        at_seq(x + step, yh, head),
                    )
                )
        along.append(hops)
    for copy in along[0]:
        copy.start()
    n_load = pltpu.make_async_copy(n_hbm, n_ref, n_load_sem)
    n_load.start()

    def arrived(step, c):
        for kind in range(2):
            dst = kv.at[8 - 4 * step + c, kind]
            remote(dst, dst, x_send.at[step - 1, kind, c], x_recv.at[step - 1, kind, c], partner).wait_recv()

    def turn(i, carry):
        cols = pl.ds(pl.multiple_of(i * HD, HD), HD)
        turned[cols, :] = n_ref[:, cols].T
        return carry

    first_src = jnp.where(yh == 0, 8, 4)
    second_src = jnp.where(yh == 0, 4, 0)
    first = [
        remote(kv.at[first_src + c], kv.at[6 + c], y_send.at[0, c], y_recv.at[0, c], across)
        for c in range(2)
    ]
    second = [
        remote(kv.at[second_src + c], kv.at[2 + c], y_send.at[1, c], y_recv.at[1, c], across)
        for c in range(2)
    ]
    for copy in local:
        copy.wait()
    for copy in swaps:
        copy.wait_recv()

    @pl.when(yh == 0)
    def _():
        for copy in first:
            copy.start()

    n_load.wait()
    lax.fori_loop(0, D // HD, turn, 0)
    n_local = pltpu.make_async_copy(turned, nt_out.at[core], n_sem)
    n_swap = remote(turned, nt_out.at[core], n_send, n_recv, partner)
    for c in range(2):
        arrived(1, c)

        @pl.when(yh == 0)
        def _():
            second[c].start()

        @pl.when(yh == 1)
        def _():
            first[c].start()

    for copy in along[1]:
        copy.start()
    n_local.start()
    n_swap.start()
    for c in range(2):
        arrived(2, c)

        @pl.when(yh == 1)
        def _():
            second[c].start()

    n_local.wait()
    n_swap.wait()
    for copy in first + second:
        copy.wait()
    for copy in swaps + along[0] + along[1]:
        copy.wait_send()


def gather(queries, keys, values, grads, normed):
    hbm = pl.BlockSpec(memory_space=pltpu.HBM)
    dma = pltpu.SemaphoreType.DMA
    return pl.pallas_call(
        gather_kernel,
        out_shape=(
            jax.ShapeDtypeStruct((2, TOK, 2 * HD), BF),
            jax.ShapeDtypeStruct((2, TOK, 2 * HD), BF),
            jax.ShapeDtypeStruct((NB, 2, TOK, HD), BF),
            jax.ShapeDtypeStruct((2, D, TOK), BF),
        ),
        in_specs=[hbm] * 5,
        out_specs=(hbm,) * 4,
        scratch_shapes=[
            pltpu.VMEM((TOK, D), BF), pltpu.VMEM((D, TOK), BF),
            dma, dma((4,)), dma((4,)), dma((4,)), dma((2, 2, 2)), dma((2, 2, 2)),
            dma((2, 2)), dma((2, 2)), dma, dma, dma,
        ],
        compiler_params=pltpu.CompilerParams(
            collective_id=0, has_side_effects=True, vmem_limit_bytes=60 << 20
        ),
        name="gather",
    )(queries, grads, keys, values, normed)


STEP = 8
PIECES = 4 * NB
EMPTY = PIECES
OWN = PIECES + STEP


def attend_kernel(
    valid, base, q, g, kv_hbm, cos, sin, dq_out, dkv_out, own_out,
    kv, e_s, w_s, kt_s, vt_s, o_acc, dq_acc, dk_acc, dv_acc, listed, sem,
):
    first_shard = base[0]
    load = pltpu.make_async_copy(kv_hbm, kv.at[pl.ds(0, NB)], sem)
    load.start()
    dk_acc[...] = jnp.zeros_like(dk_acc)
    dv_acc[...] = jnp.zeros_like(dv_acc)
    for k in range(STEP):
        kv[NB + k // 4, 0, k % 4] = jnp.zeros((HD, HD), BF)
        kv[NB + k // 4, 1, k % 4] = jnp.zeros((HD, HD), BF)
        kt_s[EMPTY + k] = jnp.zeros((HD, HD), BF)
        vt_s[EMPTY + k] = jnp.zeros((HD + 16, HD), BF)
    load.wait()

    def valid_of(b):
        return valid[jnp.maximum(first_shard + b, 0)]

    def turn(b, carry):
        for k in range(4):
            live = lax.broadcasted_iota(jnp.int32, (HD + 16, HD), 1) + k * HD < valid_of(b)
            k_t = kv[b, 0, k].T
            v_t = jnp.concatenate([kv[b, 1, k].T, jnp.ones((16, HD), BF)], axis=0)
            kt_s[4 * b + k] = jnp.where(live[:HD], k_t.astype(F32), 0.0).astype(BF)
            vt_s[4 * b + k] = jnp.where(live, v_t.astype(F32), 0.0).astype(BF)

            @pl.when(b >= 8)
            def _():
                kt_s[OWN + 4 * (b - 8) + k] = k_t
                vt_s[OWN + 4 * (b - 8) + k] = v_t

        return carry

    lax.fori_loop(0, NB, turn, 0)
    key_iota = lax.broadcasted_iota(jnp.int32, (TILE, 2 * TILE), 0)
    query_iota = lax.rem(lax.broadcasted_iota(jnp.int32, (TILE, 2 * TILE), 1), TILE)

    def query_tile(i, carry):
        r, qt = i // 2, lax.rem(i, 2)
        q_valid = valid_of(8 + r)
        q_rows = pl.ds(pl.multiple_of(qt * TILE, TILE), TILE)
        lanes = q_rows

        @pl.when(qt * TILE >= q_valid)
        def _():
            dq_out[r, :, lanes] = jnp.zeros((2 * HD, TILE), BF)

        @pl.when(qt * TILE < q_valid)
        def _():
            def note(t, count):
                j, k = t // 4, lax.rem(t, 4)
                b = r + j
                wanted = (
                    (first_shard + b >= 0)
                    & (k * HD < valid_of(b))
                    & jnp.logical_not((j == 0) & (k < 2 * qt + 2))
                    & jnp.logical_not((j == 8) & (k >= 2 * qt))
                )
                listed[count] = jnp.where(wanted, 4 * b + k, EMPTY)
                return count + wanted.astype(jnp.int32)

            count = lax.fori_loop(0, 36, note, 0)
            for extra in range(STEP - 1):
                listed[count + extra] = EMPTY + extra
            steps = (count + STEP - 1) // STEP
            doubles = steps // 2

            q_two = q[r, q_rows, :]
            g_two = g[r, q_rows, :]
            q_rows2 = jnp.concatenate([q_two[:, :HD], q_two[:, HD:]], axis=0)
            q_t = q_rows2.T

            def keys_of(kind, pieces):
                return jnp.concatenate([kv[p // 4, kind, lax.rem(p, 4)] for p in pieces], axis=0)

            def turned_of(ref, pieces):
                return jnp.concatenate([ref[p] for p in pieces], axis=1)

            def forward(pieces, turned, slot, mask):
                parts = []
                for n in range(0, len(pieces), 2):
                    keys = keys_of(0, pieces[n : n + 2])
                    rows = pl.ds(pl.multiple_of(slot + n * HD, TILE), TILE)
                    heads = []
                    for head in range(2):
                        cols = slice(head * TILE, (head + 1) * TILE)
                        th = jnp.tanh(nn(keys, q_t[:, cols]) * (SCALE / SOFT_CAP))
                        e = jnp.exp2(th * (SOFT_CAP * LOG2E))
                        if mask is not None:
                            e = jnp.where(mask[n // 2][:, cols], e, 0.0)
                        eb = e.astype(BF)
                        e_s[rows, cols] = eb
                        w_s[rows, cols] = (e * (1.0 - th * th)).astype(BF)
                        heads.append(eb)
                    parts.append(heads)
                for head in range(2):
                    cols = slice(head * TILE, (head + 1) * TILE)
                    column = jnp.concatenate([p[head] for p in parts], axis=0)
                    o_acc[:, cols] += nn(turned_of(vt_s, turned), column)

            gap = query_iota - key_iota
            key_pos = key_iota + qt * TILE
            oldest_there = first_shard + r >= 0
            edge_mask = (
                gap + 8 * TOK < WINDOW,
                (gap >= 0) & ((key_pos < q_valid) | (gap == 0)),
            )
            old = jnp.where(oldest_there, 4 * r + 2 * qt, EMPTY)
            own = 4 * (8 + r) + 2 * qt
            edge = (old, old + 1, own, own + 1)
            edge_turned = (old, old + 1, OWN + 4 * r + 2 * qt, OWN + 4 * r + 2 * qt + 1)
            o_acc[...] = jnp.zeros_like(o_acc)
            forward(edge, edge_turned, 0, edge_mask)

            def forward_step(width, n, carry):
                pieces = tuple(listed[n * width + m] for m in range(width))
                forward(pieces, pieces, (4 + n * width) * HD, None)
                return carry

            lax.fori_loop(0, doubles, functools.partial(forward_step, 2 * STEP), 0)
            lax.fori_loop(2 * doubles, steps, functools.partial(forward_step, STEP), 0)
            inv = 1.0 / o_acc[HD : HD + 1, :]
            g_rows2 = jnp.concatenate([g_two[:, :HD], g_two[:, HD:]], axis=0).astype(F32)
            live = query_iota[:1, :] + qt * TILE < q_valid
            g_t = jnp.where(live, g_rows2.T, 0.0) * inv
            delta = jnp.sum(g_t * o_acc[:HD, :], axis=0, keepdims=True) * inv
            gs_t = g_t.astype(BF)
            gs = g_t.T.astype(BF)
            dq_acc[...] = jnp.zeros_like(dq_acc)

            def backward(pieces, turned, slot):
                rows = pl.ds(pl.multiple_of(slot, TILE), len(pieces) * HD)
                columns = []
                for head in range(2):
                    cols = slice(head * TILE, (head + 1) * TILE)
                    parts = []
                    for n in range(0, len(pieces), 2):
                        part = pl.ds(pl.multiple_of(slot + n * HD, TILE), TILE)
                        dp = nn(keys_of(1, pieces[n : n + 2]), gs_t[:, cols])
                        parts.append((w_s[part, cols].astype(F32) * (dp - delta[:, cols])).astype(BF))
                    columns.append(jnp.concatenate(parts, axis=0))
                ds = jnp.concatenate(columns, axis=1)
                dq_acc[...] += nn(turned_of(kt_s, turned), ds)
                dk = nn(ds, q_rows2)
                dv = nn(e_s[rows, :], gs)
                for n, p in enumerate(pieces):
                    dk_acc[p] += dk[n * HD : (n + 1) * HD]
                    dv_acc[p] += dv[n * HD : (n + 1) * HD]

            backward(edge, edge_turned, 0)

            def backward_step(width, n, carry):
                pieces = tuple(listed[n * width + m] for m in range(width))
                backward(pieces, pieces, (4 + n * width) * HD)
                return carry

            lax.fori_loop(0, doubles, functools.partial(backward_step, 2 * STEP), 0)
            lax.fori_loop(2 * doubles, steps, functools.partial(backward_step, STEP), 0)
            dq = dq_acc[...] * SCALE
            c, s = cos[r, :, lanes], sin[r, :, lanes]
            for head in range(2):
                a = dq[: HD // 2, head * TILE : (head + 1) * TILE]
                z = dq[HD // 2 :, head * TILE : (head + 1) * TILE]
                dq_out[r, head * HD : head * HD + HD // 2, lanes] = (a * c + z * s).astype(BF)
                dq_out[r, head * HD + HD // 2 : (head + 1) * HD, lanes] = (z * c - a * s).astype(BF)

        return carry

    lax.fori_loop(0, 4, query_tile, 0)

    def result(ref, b, k, scale):
        live = lax.broadcasted_iota(jnp.int32, (HD, HD), 0) + k * HD < valid_of(b)
        return jnp.where(live, ref[4 * b + k] * scale, 0.0)

    def give(b, carry):
        for k in range(4):
            rows = slice(k * HD, (k + 1) * HD)
            dkv_out[b, 0, rows, :] = result(dk_acc, b, k, SCALE).astype(BF)
            dkv_out[b, 1, rows, :] = result(dv_acc, b, k, 1.0).astype(BF)
        return carry

    lax.fori_loop(0, 8, give, 0)
    for r in range(2):
        for k in range(4):
            rows = slice(k * HD, (k + 1) * HD)
            own_out[r, 0, rows, :] = result(dk_acc, 8 + r, k, SCALE)
            own_out[r, 1, rows, :] = result(dv_acc, 8 + r, k, 1.0)


def attend(valid_len, base, qx, gx, kv, cos, sin):
    vmem = pl.BlockSpec(memory_space=pltpu.VMEM)
    smem = pl.BlockSpec(memory_space=pltpu.SMEM)
    return pl.pallas_call(
        attend_kernel,
        out_shape=(
            jax.ShapeDtypeStruct((2, 2 * HD, TOK), BF),
            jax.ShapeDtypeStruct((8, 2, TOK, HD), BF),
            jax.ShapeDtypeStruct((2, 2, TOK, HD), F32),
        ),
        in_specs=[smem, smem, vmem, vmem, pl.BlockSpec(memory_space=pltpu.HBM), vmem, vmem],
        out_specs=(vmem,) * 3,
        scratch_shapes=[
            pltpu.VMEM((NB + STEP // 4, 2, 4, HD, HD), BF),
            pltpu.VMEM((44 * HD, 2 * TILE), BF),
            pltpu.VMEM((44 * HD, 2 * TILE), BF),
            pltpu.VMEM((OWN + 8, HD, HD), BF),
            pltpu.VMEM((OWN + 8, HD + 16, HD), BF),
            pltpu.VMEM((HD + 16, 2 * TILE), F32),
            pltpu.VMEM((HD, 2 * TILE), F32),
            pltpu.VMEM((PIECES + STEP, HD, HD), F32),
            pltpu.VMEM((PIECES + STEP, HD, HD), F32),
            pltpu.SMEM((48,), jnp.int32),
            pltpu.SemaphoreType.DMA,
        ],
        compiler_params=pltpu.CompilerParams(vmem_limit_bytes=58 << 20),
        name="attend",
    )(valid_len, base, qx, gx, kv.reshape(NB, 2, 4, HD, HD), cos, sin)


PIECE = 256


def finish_kernel(
    dq, dkv, own_hbm, turned_hbm, wq, wk, wv, cos, sin, gx_out, gw_out,
    own, n_buf, w_buf, t_buf, d_buf, y_buf, x_buf, near, far,
    xs, xr, zs, zr, xy, zy, half_buf,
    load_sem, dq_sems, dk_sems, y_sems, x_sems, ring_send, ring_recv, pair_sems, core_sems,
):
    x, yh, core, z, yl = here()
    other = 1 - core
    partner = at_seq(x, yh, other)
    across = at_seq(x, 1 - yh, core)
    beside = at_head(z, 1 - yl)
    x_next, x_prev, x_far = at_seq(x + 1, yh, core), at_seq(x - 1, yh, core), at_seq(x + 2, yh, core)
    z_next, z_prev = at_head(z + 1, yl), at_head(z - 1, yl)
    greet([partner, across, beside, x_next, x_prev, x_far, z_next, z_prev])

    y_copies = [
        remote(dkv.at[pl.ds(6 - 4 * i, 2)], y_buf.at[i], y_sems.at[0, i], y_sems.at[1, i], across)
        for i in range(2)
    ]
    for copy in y_copies:
        copy.start()
    pairs = [
        (dkv.at[pl.ds(0, 2)], far),
        (dkv.at[pl.ds(4, 2)], near),
        (dq.at[0], t_buf.at[: 2 * HD, :TOK]),
        (dq.at[1], t_buf.at[: 2 * HD, TOK:]),
        (turned_hbm.at[0], n_buf.at[:, :TOK]),
        (turned_hbm.at[1], n_buf.at[:, TOK:]),
        (own_hbm, own),
        (wq, w_buf.at[:, : 4 * HD]),
        (wk, w_buf.at[:, 4 * HD : 6 * HD]),
        (wv, w_buf.at[:, 6 * HD :]),
    ]
    loads = [pltpu.make_async_copy(src, dst, load_sem.at[i]) for i, (src, dst) in enumerate(pairs)]
    for copy in loads:
        copy.start()
    head_rows = pl.ds(pl.multiple_of(core * 2 * HD, 2 * HD), 2 * HD)
    dq_swap = remote(dq.at[other], d_buf.at[head_rows], dq_sems.at[0], dq_sems.at[1], partner)
    dq_keep = pltpu.make_async_copy(dq.at[core], d_buf.at[head_rows], dq_sems.at[2])
    back_near = remote(near, x_buf.at[0], x_sems.at[0, 0], x_sems.at[1, 0], x_prev)
    back_far = remote(far, x_buf.at[1], x_sems.at[0, 1], x_sems.at[1, 1], x_far)
    loads[0].wait()

    @pl.when(yh == 0)
    def _():
        back_far.start()

    dq_swap.start()
    dq_keep.start()
    for copy in loads[1:6]:
        copy.wait()

    send, recv = (xs, zs), (xr, zr)
    ahead, behind = (x_next, z_next), (x_prev, z_prev)
    place = (x, z)

    def term(axis, piece, rows):
        part = slice(piece * PIECE, (piece + 1) * PIECE)
        if axis == 0:
            return nt(n_buf[rows, :], t_buf[part, :])
        return nn(w_buf[rows, :], d_buf[:, part])

    def compute(job, slot, step):
        axis, piece = job
        first_row = lax.rem(place[axis] + step, 4) * CHUNK

        def one(half, carry):
            to = pl.ds(pl.multiple_of(half * HALF, HALF), HALF)
            rows = pl.ds(pl.multiple_of(first_row + half * HALF, HALF), HALF)
            send[axis][piece, slot, to, :] = term(axis, piece, rows).astype(BF)
            return carry

        lax.fori_loop(0, 2, one, 0)

    def ring(job):
        axis, piece = job
        out, come = send[axis].at[piece], recv[axis].at[piece]
        top, low = pl.ds(0, HALF), pl.ds(HALF, HALF)
        spans = (
            (out.at[0, top], come.at[0, top], ahead[axis]),
            (out.at[0, low], come.at[0, low], behind[axis]),
            (out.at[1], come.at[1], ahead[axis]),
            (out.at[2], come.at[2], behind[axis]),
        )
        return [
            remote(src, dst, ring_send.at[axis, piece, i], ring_recv.at[axis, piece, i], device)
            for i, (src, dst, device) in enumerate(spans)
        ]

    x0, x1, z0, z1 = jobs = ((0, 0), (0, 1), (1, 0), (1, 1))
    rings = {job: ring(job) for job in jobs}

    def launch(job):
        compute(job, 0, 2)
        rings[job][0].start()
        rings[job][1].start()

    def prepare(job):
        compute(job, 1, 1)
        compute(job, 2, 3)

    def relay(job):
        axis, piece = job
        for way, rows in ((0, slice(0, HALF)), (1, slice(HALF, CHUNK))):
            rings[job][way].wait()
            mine = send[axis][piece, 1 + way, rows, :].astype(F32)
            send[axis][piece, 1 + way, rows, :] = (
                mine + recv[axis][piece, 0, rows, :].astype(F32)
            ).astype(BF)
            rings[job][2 + way].start()

    side, side_device, pair_buf = (yh, yl), (across, beside), (xy, zy)

    def pair(job):
        axis, piece = job
        buf = pair_buf[axis].at[piece]
        return remote(
            buf.at[0], buf.at[1], pair_sems.at[0, axis, piece], pair_sems.at[1, axis, piece], side_device[axis]
        )

    pairs_of = {job: pair(job) for job in jobs}

    def cross(job):
        axis, piece = job
        rings[job][2].wait()
        rings[job][3].wait()

        def summed(half):
            rows = pl.ds(pl.multiple_of(half * HALF, HALF), HALF)
            return (
                send[axis][piece, 3, rows, :].astype(F32)
                + recv[axis][piece, 1, rows, :].astype(F32)
                + recv[axis][piece, 2, rows, :].astype(F32)
            ).astype(BF)

        pair_buf[axis][piece, 0] = summed(1 - side[axis])
        pairs_of[job].start()
        pair_buf[axis][piece, 2] = summed(side[axis])

    def total_of(job):
        axis, piece = job
        pairs_of[job].wait()
        return (pair_buf[axis][piece, 1].astype(F32) + pair_buf[axis][piece, 2].astype(F32)).astype(BF)

    my_rows = pl.ds(pl.multiple_of(core * QTR, QTR), QTR)
    its_rows = pl.ds(pl.multiple_of(other * QTR, QTR), QTR)
    lasts = [
        remote(half_buf.at[piece, its_rows], gw_out.at[piece, core], core_sems.at[0, piece], core_sems.at[1, piece], partner)
        for piece in range(2)
    ]

    def swap(piece):
        half_buf[piece] = total_of((0, piece))
        lasts[piece].start()
        gw_out[piece, core] = half_buf[piece, my_rows, :]

    launch(x0)
    prepare(x0)
    relay(x0)
    compute(x0, 3, 0)

    def add_to(ref, index):
        ref[...] = (ref[...].astype(F32) + y_buf[index].astype(F32)).astype(BF)

    y_copies[0].wait()

    @pl.when(yh == 1)
    def _():
        add_to(near, 0)
        back_near.start()

    y_copies[1].wait()

    @pl.when(yh == 0)
    def _():
        add_to(near, 1)
        back_near.start()

    @pl.when(yh == 1)
    def _():
        add_to(far, 1)
        back_far.start()

    keep = (yh == 0).astype(F32)
    for copy in loads[6:]:
        copy.wait()
    dq_keep.wait()
    dq_swap.wait()
    back_near.wait()
    back_far.wait()
    for r in range(2):
        for kind in range(2):
            total = (
                own[r, kind]
                + y_buf[0, r, kind].astype(F32) * keep
                + x_buf[0, r, kind].astype(F32)
                + x_buf[1, r, kind].astype(F32)
            ).T
            if kind == 0:
                a, b = total[: HD // 2, :], total[HD // 2 :, :]
                c, s = cos[r], sin[r]
                total = jnp.concatenate([a * c + b * s, b * c - a * s], axis=0)
            t_buf[(2 + kind) * HD : (3 + kind) * HD, r * TOK : (r + 1) * TOK] = total.astype(BF)
    dk_swaps = []
    its_cols = pl.ds(pl.multiple_of(other * TOK, TOK), TOK)
    my_cols = pl.ds(pl.multiple_of(core * TOK, TOK), TOK)
    for kind in range(2):
        rows = pl.ds(pl.multiple_of((4 + 2 * kind) * HD + core * HD, HD), HD)
        mine = pl.ds((2 + kind) * HD, HD)
        copy = remote(
            t_buf.at[mine, its_cols], d_buf.at[rows], dk_sems.at[0, kind], dk_sems.at[1, kind], partner
        )
        copy.start()
        dk_swaps.append(copy)
        d_buf[rows, :] = t_buf[mine, my_cols]
    for copy in dk_swaps:
        copy.wait()

    launch(z0)
    launch(z1)
    launch(x1)
    cross(x0)
    for job in (z0, z1, x1):
        prepare(job)
        relay(job)
    for job in (z0, z1, x1):
        compute(job, 3, 0)
    swap(0)
    for job in (z0, x1, z1):
        cross(job)
    gx_out[:, :PIECE] = total_of(z0)
    swap(1)
    gx_out[:, PIECE:] = total_of(z1)
    for copy in lasts:
        copy.wait()


def finish(dq, dkv, own, turned, wq, wk, wv, cos, sin):
    vmem = pl.BlockSpec(memory_space=pltpu.VMEM)
    hbm = pl.BlockSpec(memory_space=pltpu.HBM)
    any_space = pl.BlockSpec(memory_space=pl.ANY)
    dma = pltpu.SemaphoreType.DMA
    return pl.pallas_call(
        finish_kernel,
        out_shape=(
            jax.ShapeDtypeStruct((HALF, TOK), BF),
            jax.ShapeDtypeStruct((2, 2, QTR, PIECE), BF),
        ),
        in_specs=[any_space] * 3 + [hbm] * 4 + [vmem, vmem],
        out_specs=(vmem,) * 2,
        scratch_shapes=[
            pltpu.VMEM((2, 2, TOK, HD), F32),
            pltpu.VMEM((D, 2 * TOK), BF),
            pltpu.VMEM((D, 8 * HD), BF),
            pltpu.VMEM((4 * HD, 2 * TOK), BF),
            pltpu.VMEM((8 * HD, TOK), BF),
            pltpu.VMEM((2, 2, 2, TOK, HD), BF),
            pltpu.VMEM((2, 2, 2, TOK, HD), BF),
            pltpu.VMEM((2, 2, TOK, HD), BF),
            pltpu.VMEM((2, 2, TOK, HD), BF),
            pltpu.VMEM((2, 4, CHUNK, PIECE), BF),
            pltpu.VMEM((2, 3, CHUNK, PIECE), BF),
            pltpu.VMEM((2, 4, CHUNK, PIECE), BF),
            pltpu.VMEM((2, 3, CHUNK, PIECE), BF),
            pltpu.VMEM((2, 3, HALF, PIECE), BF),
            pltpu.VMEM((2, 3, HALF, PIECE), BF),
            pltpu.VMEM((2, HALF, PIECE), BF),
            dma((10,)), dma((3,)), dma((2, 2)), dma((2, 2)), dma((2, 2)),
            dma((2, 2, 4)), dma((2, 2, 4)), dma((2, 2, 2)), dma((2, 2)),
        ],
        compiler_params=pltpu.CompilerParams(
            collective_id=1, has_side_effects=True, vmem_limit_bytes=58 << 20
        ),
        name="finish",
    )(dq, dkv, own, turned, wq, wk, wv, cos, sin)


def emit_kernel(gx, gw, gx_out, gq_out, gk_out, gv_out):
    gx_out[...] = gx[...]
    for head in range(2):
        gq_out[:, head * 2 * HD : (head + 1) * 2 * HD] = gw[0, head]
        gk_out[:, head * HD : (head + 1) * HD] = gw[1, head, :, :HD]
        gv_out[:, head * HD : (head + 1) * HD] = gw[1, head, :, HD:]


def emit(gx, gw):
    vmem = pl.BlockSpec(memory_space=pltpu.VMEM)
    return pl.pallas_call(
        emit_kernel,
        out_shape=(
            jax.ShapeDtypeStruct((HALF, TOK), BF),
            jax.ShapeDtypeStruct((QTR, 4 * HD), BF),
            jax.ShapeDtypeStruct((QTR, 2 * HD), BF),
            jax.ShapeDtypeStruct((QTR, 2 * HD), BF),
        ),
        in_specs=[vmem] * 2,
        out_specs=(vmem,) * 4,
        name="emit",
    )(gx, gw)


def body(queries, keys, values, out_grad, normed, w_query, w_key, w_value, valid_len):
    chip = lax.axis_index("seq") // 2
    inverse_freq = ROPE_BASE ** (-(jnp.arange(HD // 2, dtype=F32) * (2.0 / HD)))
    slots = (chip * 2 * TOK + jnp.arange(2 * TOK, dtype=jnp.int32)).astype(F32).reshape(2, 1, TOK)
    angles = slots * inverse_freq[None, :, None]
    cos, sin = jnp.cos(angles), jnp.sin(angles)
    base = (2 * chip - 8).astype(jnp.int32).reshape(1)
    qx, gx, kv, turned = gather(queries, keys, values, out_grad, normed)
    dq, dkv, own = attend(valid_len, base, qx, gx, kv, cos, sin)
    gx, gq, gk, gv = emit(*finish(dq, dkv, own, turned, w_query, w_key, w_value, cos, sin))
    return gx.T, gq, gk, gv


def solution(mesh):
    both = P("seq", "head")
    placed = (both, both, both, both, P("seq", None), P(None, "head"), P(None, "head"), P(None, "head"), P())
    return jax.shard_map(
        body, mesh=mesh, in_specs=placed, out_specs=(both,) * 4, check_vma=False
    )
```

time: 244 us -> 214 us (0.88); the launches traced: 244 us -> 211 us
  Pallas kernels: 225 us -> 208 us
  local copies, waits for them, and re-layouts: 16.7 us -> 0 us
    pallas_call x1 -> x2, Pallas kernels: 167 us -> 123 us  [the longest x1 121 us: finish(): pl.pallas_call(finish_kernel, out_shape=(jax.ShapeDtypeStruct((HALF, TOK)...]
    pallas_call x1, Pallas kernels: 42.6 us -> 60 us  [gather(): pl.pallas_call(gather_kernel, out_shape=(jax.ShapeDtypeStruct((2, TOK, 2...]
    unnamed x25 -> x0, local copies, waits for them, and re-layouts: 14.6 us -> none
    pallas_call x1, Pallas kernels: 15.5 us -> 25 us  [attend(): pl.pallas_call(attend_kernel, out_shape=(jax.ShapeDtypeStruct((2, 2 * HD,...]
where the time goes in v2:
time: 214 us; the launch traced here: 211 us
  Pallas kernels  208 us (97%)
    pallas_call x1, Pallas kernels, finish(): pl.pallas_call(finish_kernel, out_shape=(jax.ShapeDtypeStruct((HALF, TOK)...  121 us
    pallas_call x1, Pallas kernels, gather(): pl.pallas_call(gather_kernel, out_shape=(jax.ShapeDtypeStruct((2, TOK, 2...  60 us
    pallas_call x1, Pallas kernels, attend(): pl.pallas_call(attend_kernel, out_shape=(jax.ShapeDtypeStruct((2, 2 * HD,...  25 us

profile of v2, /device:TPU:1, one launch (start us, length us, event | category | flops | bytes accessed | tf_op | source)
XLA Modules:
  0.0 211.0 jit_solution(15825124764019681618)
XLA Ops:
  0.7 1.8 multiply_sine_fusion
  2.5 60.0 %gather.1 = (bf16[2,512,256]{2,1,0:T(8,128)(2,1)}, bf16[2,512,256]{2,1,0:T(8,128)(2,1)}, bf16[10,2,512,128]{3,2,1,0:T(8,128)(2,1)}, bf16[2,4608,512]{2,1,0:T(8,128)(2,1)}) custom-call(bf16[512,512]{1,0:T(8,128)(2,1)} %q.1, bf16[512,512]{1,0:T(8,128)(2,1)} %g.1, bf16[512,256]{1,0:T(8,128)(2,1)} %k.1, bf16[512,256]{1,0:T(8,128)(2,1)} %v.1, bf16[512,4608]{1,0:T(8,128)(2,1)} %n_hbm.1), custom_call_target="tpu_custom_call" | custom-call | tf_op jit(solution)/shard_map/gather/pallas_call | solution.py:186
  62.6 25.0 %attend.1 = (bf16[2,256,512]{2,1,0:T(8,128)(2,1)}, bf16[8,2,512,128]{3,2,1,0:T(8,128)(2,1)}, f32[2,2,512,128]{3,2,1,0:T(8,128)}) custom-call(s32[16]{0:T(128)} %valid.1, s32[1]{0:T(128)} %bitcast.base, bf16[2,512,256]{2,1,0:T(8,128)(2,1)} %get-tuple-element.17.q, bf16[2,512,256]{2,1,0:T(8,128)(2,1)} %get-tuple-element.18.g, ...), custom_call_target="tpu_custom_call" | custom-call | tf_op jit(solution)/shard_map/attend/pallas_call | solution.py:407
  87.6 121.1 %finish.1 = (bf16[576,512]{1,0:T(8,128)(2,1)}, bf16[2,2,288,256]{3,2,1,0:T(8,128)(2,1)}) custom-call(bf16[2,256,512]{2,1,0:T(8,128)(2,1)} %get-tuple-element.20.dq, bf16[8,2,512,128]{3,2,1,0:T(8,128)(2,1)} %get-tuple-element.21.dkv, f32[2,2,512,128]{3,2,1,0:T(8,128)} %get-tuple-element.22.own_hbm, bf16[2,4608,512]{2,1,0:T(8,128)(2,1)} %get-tuple-element.23.turned_hbm, ...), custom_call_target="tpu_custom_call" | custom-call | tf_op jit(solution)/shard_map/finish/pallas_call | solution.py:679
  208.7 2.3 %emit.1 = (bf16[576,512]{1,0:T(8,128)(2,1)}, bf16[288,512]{1,0:T(8,128)(2,1)}, bf16[288,256]{1,0:T(8,128)(2,1)}, bf16[288,256]{1,0:T(8,128)(2,1)}) custom-call(bf16[576,512]{1,0:T(8,128)(2,1)} %get-tuple-element.24.gx, bf16[2,2,288,256]{3,2,1,0:T(8,128)(2,1)} %get-tuple-element.25.gw), custom_call_target="tpu_custom_call" | custom-call | tf_op jit(solution)/shard_map/emit/pallas_call | solution.py:724
  (2 shorter events, 0.0 us)

commit v3 on v2

--- a/solution.py
+++ b/solution.py
@@ -63,63 +63,60 @@
 
 
 def gather_kernel(
-    q, g, k, v, n_hbm, qx, gx, kv, nt_out, n_ref, turned,
-    n_load_sem, loc_sem, swap_send, swap_recv, x_send, x_recv, y_send, y_recv, n_sem, n_send, n_recv,
+    q, g, k, v, n_hbm, qg, kv, nt_out, kv_own, qg_own, n_ref, turned,
+    n_load_sem, kv_load, qg_load, kv_loc, qg_loc, swap_send, swap_recv,
+    x_send, x_recv, y_send, y_recv, n_sem, n_send, n_recv,
 ):
     x, yh, core, _, _ = here()
     other = 1 - core
     partner = at_seq(x, yh, other)
     across = at_seq(x, 1 - yh, core)
+
+    def stage(pair, to, width, sems):
+        return [
+            pltpu.make_async_copy(
+                ref.at[:, head * width : (head + 1) * width], to.at[head, kind], sems.at[head, kind]
+            )
+            for head in range(2)
+            for kind, ref in enumerate(pair)
+        ]
+
+    kv_stage = stage((k, v), kv_own, HD, kv_load)
+    qg_stage = stage((q, g), qg_own, 2 * HD, qg_load)
+    n_load = pltpu.make_async_copy(n_hbm, n_ref, n_load_sem)
+    for copy in kv_stage + qg_stage + [n_load]:
+        copy.start()
     greet(
         [partner, across]
         + [at_seq(x + step, yh, c) for step in (1, -1, 2) for c in range(2)]
     )
-
-    def head_cols(ref, head, width):
-        return ref.at[:, pl.ds(pl.multiple_of(head * width, width), width)]
-
-    local = [
-        pltpu.make_async_copy(head_cols(k, core, HD), kv.at[8 + core, 0], loc_sem.at[0]),
-        pltpu.make_async_copy(head_cols(v, core, HD), kv.at[8 + core, 1], loc_sem.at[1]),
-        pltpu.make_async_copy(head_cols(q, core, 2 * HD), qx.at[core], loc_sem.at[2]),
-        pltpu.make_async_copy(head_cols(g, core, 2 * HD), gx.at[core], loc_sem.at[3]),
+    for copy in kv_stage:
+        copy.wait()
+    along = [
+        [
+            remote(
+                kv_own.at[head],
+                kv.at[8 - 4 * step + core],
+                x_send.at[step - 1, head],
+                x_recv.at[step - 1, core],
+                at_seq(x + step, yh, head),
+            )
+            for head in range(2)
+        ]
+        for step in (1, 2)
     ]
-    pairs = [
-        (head_cols(k, other, HD), kv.at[8 + core, 0]),
-        (head_cols(v, other, HD), kv.at[8 + core, 1]),
-        (head_cols(q, other, 2 * HD), qx.at[core]),
-        (head_cols(g, other, 2 * HD), gx.at[core]),
-    ]
-    swaps = [
-        remote(src, dst, swap_send.at[i], swap_recv.at[i], partner)
-        for i, (src, dst) in enumerate(pairs)
-    ]
-    for copy in local + swaps:
+    kv_swap = remote(kv_own.at[other], kv.at[8 + core], swap_send.at[0], swap_recv.at[0], partner)
+    kv_keep = pltpu.make_async_copy(kv_own.at[core], kv.at[8 + core], kv_loc)
+    qg_swap = remote(qg_own.at[other], qg.at[core], swap_send.at[1], swap_recv.at[1], partner)
+    qg_keep = pltpu.make_async_copy(qg_own.at[core], qg.at[core], qg_loc)
+    kv_swap.start()
+    kv_keep.start()
+    for copy in along[0] + along[1]:
         copy.start()
-    along = []
-    for step in (1, 2):
-        hops = []
-        for kind, ref in enumerate((k, v)):
-            for head in range(2):
-                hops.append(
-                    remote(
-                        ref.at[:, head * HD : (head + 1) * HD],
-                        kv.at[8 - 4 * step + core, kind],
-                        x_send.at[step - 1, kind, head],
-                        x_recv.at[step - 1, kind, core],
-                        at_seq(x + step, yh, head),
-                    )
-                )
-        along.append(hops)
-    for copy in along[0]:
-        copy.start()
-    n_load = pltpu.make_async_copy(n_hbm, n_ref, n_load_sem)
-    n_load.start()
 
     def arrived(step, c):
-        for kind in range(2):
-            dst = kv.at[8 - 4 * step + c, kind]
-            remote(dst, dst, x_send.at[step - 1, kind, c], x_recv.at[step - 1, kind, c], partner).wait_recv()
+        dst = kv.at[8 - 4 * step + c]
+        remote(dst, dst, x_send.at[step - 1, c], x_recv.at[step - 1, c], partner).wait_recv()
 
     def turn(i, carry):
         cols = pl.ds(pl.multiple_of(i * HD, HD), HD)
@@ -136,20 +133,20 @@
         remote(kv.at[second_src + c], kv.at[2 + c], y_send.at[1, c], y_recv.at[1, c], across)
         for c in range(2)
     ]
-    for copy in local:
-        copy.wait()
-    for copy in swaps:
-        copy.wait_recv()
+    kv_keep.wait()
+    kv_swap.wait_recv()
 
     @pl.when(yh == 0)
     def _():
         for copy in first:
             copy.start()
 
+    for copy in qg_stage:
+        copy.wait()
+    qg_swap.start()
+    qg_keep.start()
     n_load.wait()
-    lax.fori_loop(0, D // HD, turn, 0)
-    n_local = pltpu.make_async_copy(turned, nt_out.at[core], n_sem)
-    n_swap = remote(turned, nt_out.at[core], n_send, n_recv, partner)
+    lax.fori_loop(0, D // HD // 2, turn, 0)
     for c in range(2):
         arrived(1, c)
 
@@ -161,8 +158,9 @@
         def _():
             first[c].start()
 
-    for copy in along[1]:
-        copy.start()
+    lax.fori_loop(D // HD // 2, D // HD, turn, 0)
+    n_local = pltpu.make_async_copy(turned, nt_out.at[core], n_sem)
+    n_swap = remote(turned, nt_out.at[core], n_send, n_recv, partner)
     n_local.start()
     n_swap.start()
     for c in range(2):
@@ -174,9 +172,12 @@
 
     n_local.wait()
     n_swap.wait()
+    qg_keep.wait()
+    qg_swap.wait()
     for copy in first + second:
         copy.wait()
-    for copy in swaps + along[0] + along[1]:
+    kv_swap.wait_send()
+    for copy in along[0] + along[1]:
         copy.wait_send()
 
 
@@ -186,17 +187,19 @@
     return pl.pallas_call(
         gather_kernel,
         out_shape=(
-            jax.ShapeDtypeStruct((2, TOK, 2 * HD), BF),
-            jax.ShapeDtypeStruct((2, TOK, 2 * HD), BF),
+            jax.ShapeDtypeStruct((2, 2, TOK, 2 * HD), BF),
             jax.ShapeDtypeStruct((NB, 2, TOK, HD), BF),
             jax.ShapeDtypeStruct((2, D, TOK), BF),
         ),
         in_specs=[hbm] * 5,
-        out_specs=(hbm,) * 4,
+        out_specs=(hbm,) * 3,
         scratch_shapes=[
-            pltpu.VMEM((TOK, D), BF), pltpu.VMEM((D, TOK), BF),
-            dma, dma((4,)), dma((4,)), dma((4,)), dma((2, 2, 2)), dma((2, 2, 2)),
-            dma((2, 2)), dma((2, 2)), dma, dma, dma,
+            pltpu.VMEM((2, 2, TOK, HD), BF),
+            pltpu.VMEM((2, 2, TOK, 2 * HD), BF),
+            pltpu.VMEM((TOK, D), BF),
+            pltpu.VMEM((D, TOK), BF),
+            dma, dma((2, 2)), dma((2, 2)), dma, dma, dma((2,)), dma((2,)),
+            dma((2, 2)), dma((2, 2)), dma((2, 2)), dma((2, 2)), dma, dma, dma,
         ],
         compiler_params=pltpu.CompilerParams(
             collective_id=0, has_side_effects=True, vmem_limit_bytes=60 << 20
@@ -212,7 +215,7 @@
 
 
 def attend_kernel(
-    valid, base, q, g, kv_hbm, cos, sin, dq_out, dkv_out, own_out,
+    valid, base, qg, kv_hbm, cos, sin, dq_out, dkv_out, own_out,
     kv, e_s, w_s, kt_s, vt_s, o_acc, dq_acc, dk_acc, dv_acc, listed, sem,
 ):
     first_shard = base[0]
@@ -279,8 +282,8 @@
             steps = (count + STEP - 1) // STEP
             doubles = steps // 2
 
-            q_two = q[r, q_rows, :]
-            g_two = g[r, q_rows, :]
+            q_two = qg[r, 0, q_rows, :]
+            g_two = qg[r, 1, q_rows, :]
             q_rows2 = jnp.concatenate([q_two[:, :HD], q_two[:, HD:]], axis=0)
             q_t = q_rows2.T
 
@@ -401,7 +404,7 @@
             own_out[r, 1, rows, :] = result(dv_acc, 8 + r, k, 1.0)
 
 
-def attend(valid_len, base, qx, gx, kv, cos, sin):
+def attend(valid_len, base, qg, kv, cos, sin):
     vmem = pl.BlockSpec(memory_space=pltpu.VMEM)
     smem = pl.BlockSpec(memory_space=pltpu.SMEM)
     return pl.pallas_call(
@@ -411,7 +414,7 @@
             jax.ShapeDtypeStruct((8, 2, TOK, HD), BF),
             jax.ShapeDtypeStruct((2, 2, TOK, HD), F32),
         ),
-        in_specs=[smem, smem, vmem, vmem, pl.BlockSpec(memory_space=pltpu.HBM), vmem, vmem],
+        in_specs=[smem, smem, vmem, pl.BlockSpec(memory_space=pltpu.HBM), vmem, vmem],
         out_specs=(vmem,) * 3,
         scratch_shapes=[
             pltpu.VMEM((NB + STEP // 4, 2, 4, HD, HD), BF),
@@ -428,7 +431,7 @@
         ],
         compiler_params=pltpu.CompilerParams(vmem_limit_bytes=58 << 20),
         name="attend",
-    )(valid_len, base, qx, gx, kv.reshape(NB, 2, 4, HD, HD), cos, sin)
+    )(valid_len, base, qg, kv.reshape(NB, 2, 4, HD, HD), cos, sin)
 
 
 PIECE = 256
@@ -450,10 +453,13 @@
     greet([partner, across, beside, x_next, x_prev, x_far, z_next, z_prev])
 
     y_copies = [
-        remote(dkv.at[pl.ds(6 - 4 * i, 2)], y_buf.at[i], y_sems.at[0, i], y_sems.at[1, i], across)
+        [
+            remote(dkv.at[6 - 4 * i + r], y_buf.at[i, r], y_sems.at[0, i, r], y_sems.at[1, i, r], across)
+            for r in range(2)
+        ]
         for i in range(2)
     ]
-    for copy in y_copies:
+    for copy in y_copies[1] + y_copies[0]:
         copy.start()
     pairs = [
         (dkv.at[pl.ds(0, 2)], far),
@@ -473,13 +479,19 @@
     head_rows = pl.ds(pl.multiple_of(core * 2 * HD, 2 * HD), 2 * HD)
     dq_swap = remote(dq.at[other], d_buf.at[head_rows], dq_sems.at[0], dq_sems.at[1], partner)
     dq_keep = pltpu.make_async_copy(dq.at[core], d_buf.at[head_rows], dq_sems.at[2])
-    back_near = remote(near, x_buf.at[0], x_sems.at[0, 0], x_sems.at[1, 0], x_prev)
-    back_far = remote(far, x_buf.at[1], x_sems.at[0, 1], x_sems.at[1, 1], x_far)
+    back_near, back_far = (
+        [
+            remote(src.at[r], x_buf.at[i, r], x_sems.at[0, i, r], x_sems.at[1, i, r], device)
+            for r in range(2)
+        ]
+        for i, (src, device) in enumerate(((near, x_prev), (far, x_far)))
+    )
     loads[0].wait()
 
     @pl.when(yh == 0)
     def _():
-        back_far.start()
+        for copy in back_far:
+            copy.start()
 
     dq_swap.start()
     dq_keep.start()
@@ -590,40 +602,45 @@
         lasts[piece].start()
         gw_out[piece, core] = half_buf[piece, my_rows, :]
 
+
+    def add_to(ref, index, r):
+        ref[r] = (ref[r].astype(F32) + y_buf[index, r].astype(F32)).astype(BF)
+
+    def further(r):
+        y_copies[1][r].wait()
+
+        @pl.when(yh == 0)
+        def _():
+            add_to(near, 1, r)
+            back_near[r].start()
+
+        @pl.when(yh == 1)
+        def _():
+            add_to(far, 1, r)
+            back_far[r].start()
+
+    def nearer(r):
+        y_copies[0][r].wait()
+
+        @pl.when(yh == 1)
+        def _():
+            add_to(near, 0, r)
+            back_near[r].start()
+
     launch(x0)
     prepare(x0)
-    relay(x0)
     compute(x0, 3, 0)
-
-    def add_to(ref, index):
-        ref[...] = (ref[...].astype(F32) + y_buf[index].astype(F32)).astype(BF)
-
-    y_copies[0].wait()
-
-    @pl.when(yh == 1)
-    def _():
-        add_to(near, 0)
-        back_near.start()
-
-    y_copies[1].wait()
-
-    @pl.when(yh == 0)
-    def _():
-        add_to(near, 1)
-        back_near.start()
-
-    @pl.when(yh == 1)
-    def _():
-        add_to(far, 1)
-        back_far.start()
-
+    for r in range(2):
+        further(r)
+    for r in range(2):
+        nearer(r)
     keep = (yh == 0).astype(F32)
     for copy in loads[6:]:
         copy.wait()
     dq_keep.wait()
     dq_swap.wait()
-    back_near.wait()
-    back_far.wait()
+    for copy in back_far + back_near:
+        copy.wait()
     for r in range(2):
         for kind in range(2):
             total = (
@@ -654,6 +671,7 @@
 
     launch(z0)
     launch(z1)
+    relay(x0)
     launch(x1)
     cross(x0)
     for job in (z0, z1, x1):
@@ -701,7 +719,7 @@
             pltpu.VMEM((2, 3, HALF, PIECE), BF),
             pltpu.VMEM((2, 3, HALF, PIECE), BF),
             pltpu.VMEM((2, HALF, PIECE), BF),
-            dma((10,)), dma((3,)), dma((2, 2)), dma((2, 2)), dma((2, 2)),
+            dma((10,)), dma((3,)), dma((2, 2)), dma((2, 2, 2)), dma((2, 2, 2)),
             dma((2, 2, 4)), dma((2, 2, 4)), dma((2, 2, 2)), dma((2, 2)),
         ],
         compiler_params=pltpu.CompilerParams(
@@ -742,8 +760,8 @@
     angles = slots * inverse_freq[None, :, None]
     cos, sin = jnp.cos(angles), jnp.sin(angles)
     base = (2 * chip - 8).astype(jnp.int32).reshape(1)
-    qx, gx, kv, turned = gather(queries, keys, values, out_grad, normed)
-    dq, dkv, own = attend(valid_len, base, qx, gx, kv, cos, sin)
+    qg, kv, turned = gather(queries, keys, values, out_grad, normed)
+    dq, dkv, own = attend(valid_len, base, qg, kv, cos, sin)
     gx, gq, gk, gv = emit(*finish(dq, dkv, own, turned, w_query, w_key, w_value, cos, sin))
     return gx.T, gq, gk, gv
 

time: 214 us -> 181 us (0.85)
  Pallas kernels: 208 us -> 176 us
    pallas_call x1, Pallas kernels: 60 us -> 40.2 us  [gather(): pl.pallas_call(gather_kernel, out_shape=(jax.ShapeDtypeStruct((2, 2, TOK,...]
    pallas_call x1, Pallas kernels: 121 us -> 109 us  [finish(): pl.pallas_call(finish_kernel, out_shape=(jax.ShapeDtypeStruct((HALF, TOK)...]
where the time goes in v3:
time: 181 us; the launch traced here: 179 us
  Pallas kernels  176 us (97%)
  other arithmetic  1.85 us (1%)
    pallas_call x1, Pallas kernels, finish(): pl.pallas_call(finish_kernel, out_shape=(jax.ShapeDtypeStruct((HALF, TOK)...  109 us
    pallas_call x1, Pallas kernels, gather(): pl.pallas_call(gather_kernel, out_shape=(jax.ShapeDtypeStruct((2, 2, TOK,...  40.2 us
    pallas_call x1, Pallas kernels, attend(): pl.pallas_call(attend_kernel, out_shape=(jax.ShapeDtypeStruct((2, 2 * HD,...  25 us

profile of v3, /device:TPU:1, one launch (start us, length us, event | category | flops | bytes accessed | tf_op | source)
XLA Modules:
  0.0 178.5 jit_solution(4039767711338423779)
XLA Ops:
  0.7 1.8 %multiply_sine_fusion = (f32[2,64,512]{2,1,0:T(8,128)}, f32[2,64,512]{2,1,0:T(8,128)}) fusion(f32[64]{0:T(128)S(1)} %negate_power_fusion, f32[2,512]{1,0:T(2,128)S(1)} %add_convert_fusion), kind=kLoop, calls=%fused_computation | loop fusion | flops 65536 | bytes 528640 | tf_op jit(solution)/shard_map/sin | solution.py:761
  2.5 40.2 %gather.1 = (bf16[2,2,512,256]{3,2,1,0:T(8,128)(2,1)}, bf16[10,2,512,128]{3,2,1,0:T(8,128)(2,1)}, bf16[2,4608,512]{2,1,0:T(8,128)(2,1)}) custom-call(bf16[512,512]{1,0:T(8,128)(2,1)} %q.1, bf16[512,512]{1,0:T(8,128)(2,1)} %g.1, bf16[512,256]{1,0:T(8,128)(2,1)} %k.1, bf16[512,256]{1,0:T(8,128)(2,1)} %v.1, bf16[512,4608]{1,0:T(8,128)(2,1)} %n_hbm.1), custom_call_target="tpu_custom_call" | custom-call | tf_op jit(solution)/shard_map/gather/pallas_call | solution.py:187
  42.7 25.0 %attend.1 = (bf16[2,256,512]{2,1,0:T(8,128)(2,1)}, bf16[8,2,512,128]{3,2,1,0:T(8,128)(2,1)}, f32[2,2,512,128]{3,2,1,0:T(8,128)}) custom-call(s32[16]{0:T(128)} %valid.1, s32[1]{0:T(128)} %bitcast.base, bf16[2,2,512,256]{3,2,1,0:T(8,128)(2,1)} %get-tuple-element.16.qg, bf16[10,2,4,128,128]{4,3,2,1,0:T(8,128)(2,1)} %bitcast.3, ...), custom_call_target="tpu_custom_call" | custom-call | tf_op jit(solution)/shard_map/attend/pallas_call | solution.py:410
  67.7 108.6 %finish.1 = (bf16[576,512]{1,0:T(8,128)(2,1)}, bf16[2,2,288,256]{3,2,1,0:T(8,128)(2,1)}) custom-call(bf16[2,256,512]{2,1,0:T(8,128)(2,1)} %get-tuple-element.18.dq, bf16[8,2,512,128]{3,2,1,0:T(8,128)(2,1)} %get-tuple-element.19.dkv, f32[2,2,512,128]{3,2,1,0:T(8,128)} %get-tuple-element.20.own_hbm, bf16[2,4608,512]{2,1,0:T(8,128)(2,1)} %get-tuple-element.21.turned_hbm, ...), custom_call_target="tpu_custom_call" | custom-call | tf_op jit(solution)/shard_map/finish/pallas_call | solution.py:697
  176.3 2.3 %emit.1 = (bf16[576,512]{1,0:T(8,128)(2,1)}, bf16[288,512]{1,0:T(8,128)(2,1)}, bf16[288,256]{1,0:T(8,128)(2,1)}, bf16[288,256]{1,0:T(8,128)(2,1)}) custom-call(bf16[576,512]{1,0:T(8,128)(2,1)} %get-tuple-element.22.gx, bf16[2,2,288,256]{3,2,1,0:T(8,128)(2,1)} %get-tuple-element.23.gw), custom_call_target="tpu_custom_call" | custom-call | tf_op jit(solution)/shard_map/emit/pallas_call | solution.py:742
  (2 shorter events, 0.0 us)

commit v4 on v3

--- a/solution.py
+++ b/solution.py
@@ -25,6 +25,7 @@
 BF = jnp.bfloat16
 F32 = jnp.float32
 MESH = pl.DeviceIdType.MESH
+STEPS = (1, -1, 2)
 LOG2E = 1.4426950408889634
 
 
@@ -47,6 +48,11 @@
 
 def at_head(z, yl):
     return {"seq": lax.axis_index("seq"), "head": lax.rem(z + 4, 4) * 2 + yl}
+
+
+def at_core(z, yl, core):
+    s = lax.axis_index("seq")
+    return {"seq": s - s % 2 + core, "head": lax.rem(z + 4, 4) * 2 + yl}
 
 
 def remote(src, dst, send, recv, device):
@@ -63,11 +69,11 @@
 
 
 def gather_kernel(
-    q, g, k, v, n_hbm, qg, kv, nt_out, kv_own, qg_own, n_ref, turned,
+    q, g, k, v, n_hbm, wk, wv, qg, kv, nt_out, w_all, kv_own, qg_own, n_ref, turned,
     n_load_sem, kv_load, qg_load, kv_loc, qg_loc, swap_send, swap_recv,
-    x_send, x_recv, y_send, y_recv, n_sem, n_send, n_recv,
+    x_send, x_recv, y_send, y_recv, n_sem, n_send, n_recv, w_loc, w_send, w_recv, w_pass, w_get,
 ):
-    x, yh, core, _, _ = here()
+    x, yh, core, z, yl = here()
     other = 1 - core
     partner = at_seq(x, yh, other)
     across = at_seq(x, 1 - yh, core)
@@ -89,6 +95,7 @@
     greet(
         [partner, across]
         + [at_seq(x + step, yh, c) for step in (1, -1, 2) for c in range(2)]
+        + [at_head(z + step, yl) for step in STEPS]
     )
     for copy in kv_stage:
         copy.wait()
@@ -141,6 +148,20 @@
         for copy in first:
             copy.start()
 
+    part = pl.ds(pl.multiple_of(core * HALF, HALF), HALF)
+    w_keep, w_out, w_on = [], [], []
+    for kind, ref in enumerate((wk, wv)):
+        own_rows = pl.ds(pl.multiple_of(z * CHUNK, CHUNK), CHUNK)
+        w_keep.append(pltpu.make_async_copy(ref.at[own_rows], w_all.at[z, kind], w_loc.at[kind]))
+        for i, step in enumerate(STEPS):
+            rows = pl.ds(pl.multiple_of(lax.rem(z + 4 + step, 4) * CHUNK + core * HALF, HALF), HALF)
+            w_out.append(
+                remote(ref.at[rows], w_all.at[z, kind, part], w_send.at[kind, i], w_recv.at[kind, i], at_head(z + step, yl))
+            )
+            come = w_all.at[lax.rem(z + 4 - step, 4), kind, part]
+            w_on.append(remote(come, come, w_pass.at[kind, i], w_get.at[kind, i], partner))
+    for copy in w_out + w_keep:
+        copy.start()
     for copy in qg_stage:
         copy.wait()
     qg_swap.start()
@@ -170,18 +191,23 @@
         def _():
             second[c].start()
 
+    for out, on in zip(w_out, w_on):
+        out.wait()
+        on.start()
     n_local.wait()
     n_swap.wait()
     qg_keep.wait()
     qg_swap.wait()
     for copy in first + second:
         copy.wait()
+    for copy in w_on + w_keep:
+        copy.wait()
     kv_swap.wait_send()
     for copy in along[0] + along[1]:
         copy.wait_send()
 
 
-def gather(queries, keys, values, grads, normed):
+def gather(queries, keys, values, grads, normed, wk, wv):
     hbm = pl.BlockSpec(memory_space=pltpu.HBM)
     dma = pltpu.SemaphoreType.DMA
     return pl.pallas_call(
@@ -190,9 +216,10 @@
             jax.ShapeDtypeStruct((2, 2, TOK, 2 * HD), BF),
             jax.ShapeDtypeStruct((NB, 2, TOK, HD), BF),
             jax.ShapeDtypeStruct((2, D, TOK), BF),
+            jax.ShapeDtypeStruct((4, 2, CHUNK, 2 * HD), BF),
         ),
-        in_specs=[hbm] * 5,
-        out_specs=(hbm,) * 3,
+        in_specs=[hbm] * 7,
+        out_specs=(hbm,) * 4,
         scratch_shapes=[
             pltpu.VMEM((2, 2, TOK, HD), BF),
             pltpu.VMEM((2, 2, TOK, 2 * HD), BF),
@@ -200,12 +227,13 @@
             pltpu.VMEM((D, TOK), BF),
             dma, dma((2, 2)), dma((2, 2)), dma, dma, dma((2,)), dma((2,)),
             dma((2, 2)), dma((2, 2)), dma((2, 2)), dma((2, 2)), dma, dma, dma,
+            dma((2,)), dma((2, 3)), dma((2, 3)), dma((2, 3)), dma((2, 3)),
         ],
         compiler_params=pltpu.CompilerParams(
             collective_id=0, has_side_effects=True, vmem_limit_bytes=60 << 20
         ),
         name="gather",
-    )(queries, grads, keys, values, normed)
+    )(queries, grads, keys, values, normed, wk, wv)
 
 
 STEP = 8
@@ -438,10 +466,10 @@
 
 
 def finish_kernel(
-    dq, dkv, own_hbm, turned_hbm, wq, wk, wv, cos, sin, gx_out, gw_out,
-    own, n_buf, w_buf, t_buf, d_buf, y_buf, x_buf, near, far,
+    dq, dkv, own_hbm, turned_hbm, wq, w_all, cos, sin, gx_out, gw_out,
+    own, n_buf, w_buf, wkv_buf, t_buf, d_buf, dkv_t, g_buf, y_buf, x_buf, near, far,
     xs, xr, zs, zr, xy, zy, half_buf,
-    load_sem, dq_sems, dk_sems, y_sems, x_sems, ring_send, ring_recv, pair_sems, core_sems,
+    load_sem, dq_sems, dk_sems, y_sems, x_sems, ring_send, ring_recv, pair_sems, core_sems, g_send, g_recv,
 ):
     x, yh, core, z, yl = here()
     other = 1 - core
@@ -450,7 +478,8 @@
     beside = at_head(z, 1 - yl)
     x_next, x_prev, x_far = at_seq(x + 1, yh, core), at_seq(x - 1, yh, core), at_seq(x + 2, yh, core)
     z_next, z_prev = at_head(z + 1, yl), at_head(z - 1, yl)
-    greet([partner, across, beside, x_next, x_prev, x_far, z_next, z_prev])
+    round_z = [[at_core(z + step, yl, c) for c in range(2)] for step in STEPS]
+    greet([partner, across, beside, x_next, x_prev, x_far] + sum(round_z, []))
 
     y_copies = [
         [
@@ -464,14 +493,16 @@
     pairs = [
         (dkv.at[pl.ds(0, 2)], far),
         (dkv.at[pl.ds(4, 2)], near),
+        (wq, w_buf),
         (dq.at[0], t_buf.at[: 2 * HD, :TOK]),
         (dq.at[1], t_buf.at[: 2 * HD, TOK:]),
         (turned_hbm.at[0], n_buf.at[:, :TOK]),
         (turned_hbm.at[1], n_buf.at[:, TOK:]),
         (own_hbm, own),
-        (wq, w_buf.at[:, : 4 * HD]),
-        (wk, w_buf.at[:, 4 * HD : 6 * HD]),
-        (wv, w_buf.at[:, 6 * HD :]),
+    ] + [
+        (w_all.at[i, kind], wkv_buf.at[i, :, kind * 2 * HD : (kind + 1) * 2 * HD])
+        for i in range(4)
+        for kind in range(2)
     ]
     loads = [pltpu.make_async_copy(src, dst, load_sem.at[i]) for i, (src, dst) in enumerate(pairs)]
     for copy in loads:
@@ -495,8 +526,10 @@
 
     dq_swap.start()
     dq_keep.start()
-    for copy in loads[1:6]:
+    for copy in loads[1:3]:
         copy.wait()
+    dq_keep.wait()
+    dq_swap.wait()
 
     send, recv = (xs, zs), (xr, zr)
     ahead, behind = (x_next, z_next), (x_prev, z_prev)
@@ -568,6 +601,15 @@
 
     pairs_of = {job: pair(job) for job in jobs}
 
+    def keys_part(piece, rows):
+        total = jnp.zeros((HALF, PIECE), F32)
+        for i in range(4):
+            found = [
+                g_buf[i, head, piece, kind * HD : (kind + 1) * HD, :] for kind in range(2) for head in range(2)
+            ]
+            total += nn(wkv_buf[i, rows, :], jnp.concatenate(found, axis=0))
+        return total
+
     def cross(job):
         axis, piece = job
         rings[job][2].wait()
@@ -575,11 +617,14 @@
 
         def summed(half):
             rows = pl.ds(pl.multiple_of(half * HALF, HALF), HALF)
-            return (
+            total = (
                 send[axis][piece, 3, rows, :].astype(F32)
                 + recv[axis][piece, 1, rows, :].astype(F32)
                 + recv[axis][piece, 2, rows, :].astype(F32)
-            ).astype(BF)
+            )
+            if axis == 1:
+                total += keys_part(piece, rows)
+            return total.astype(BF)
 
         pair_buf[axis][piece, 0] = summed(1 - side[axis])
         pairs_of[job].start()
@@ -627,18 +672,23 @@
             add_to(near, 0, r)
             back_near[r].start()
 
+    launch(z0)
+    launch(z1)
+    prepare(z0)
+    prepare(z1)
+    for r in range(2):
+        further(r)
+    relay(z0)
+    relay(z1)
+    for r in range(2):
+        nearer(r)
+    for copy in loads[3:]:
+        copy.wait()
     launch(x0)
     prepare(x0)
-    compute(x0, 3, 0)
-    for r in range(2):
-        further(r)
-    for r in range(2):
-        nearer(r)
+    for job in (z0, z1, x0):
+        compute(job, 3, 0)
     keep = (yh == 0).astype(F32)
-    for copy in loads[6:]:
-        copy.wait()
-    dq_keep.wait()
-    dq_swap.wait()
     for copy in back_far + back_near:
         copy.wait()
     for r in range(2):
@@ -653,43 +703,57 @@
                 a, b = total[: HD // 2, :], total[HD // 2 :, :]
                 c, s = cos[r], sin[r]
                 total = jnp.concatenate([a * c + b * s, b * c - a * s], axis=0)
-            t_buf[(2 + kind) * HD : (3 + kind) * HD, r * TOK : (r + 1) * TOK] = total.astype(BF)
-    dk_swaps = []
-    its_cols = pl.ds(pl.multiple_of(other * TOK, TOK), TOK)
-    my_cols = pl.ds(pl.multiple_of(core * TOK, TOK), TOK)
-    for kind in range(2):
-        rows = pl.ds(pl.multiple_of((4 + 2 * kind) * HD + core * HD, HD), HD)
-        mine = pl.ds((2 + kind) * HD, HD)
-        copy = remote(
-            t_buf.at[mine, its_cols], d_buf.at[rows], dk_sems.at[0, kind], dk_sems.at[1, kind], partner
-        )
-        copy.start()
-        dk_swaps.append(copy)
-        d_buf[rows, :] = t_buf[mine, my_cols]
-    for copy in dk_swaps:
-        copy.wait()
-
-    launch(z0)
-    launch(z1)
+            total = total.astype(BF)
+            t_buf[(2 + kind) * HD : (3 + kind) * HD, r * TOK : (r + 1) * TOK] = total
+            for piece in range(2):
+                dkv_t[r, piece, kind * HD : (kind + 1) * HD, :] = total[:, piece * PIECE : (piece + 1) * PIECE]
+    spread = [
+        [
+            remote(dkv_t.at[r, piece], g_buf.at[z, core, piece], g_send.at[i, r, piece], g_recv.at[i, core, piece], round_z[i][r])
+            for i in range(3)
+            for r in range(2)
+        ]
+        for piece in range(2)
+    ]
+    kin = [
+        remote(dkv_t.at[other, piece], g_buf.at[z, core, piece], dk_sems.at[0, piece], dk_sems.at[1, piece], partner)
+        for piece in range(2)
+    ]
+    for piece in range(2):
+        for copy in spread[piece] + [kin[piece]]:
+            copy.start()
+        g_buf[z, core, piece] = dkv_t[core, piece]
+
+    def gathered(piece):
+        kin[piece].wait()
+        for i, step in enumerate(STEPS):
+            for head in range(2):
+                come = g_buf.at[lax.rem(z + 4 - step, 4), head, piece]
+                remote(come, come, g_send.at[i, head, piece], g_recv.at[i, head, piece], partner).wait_recv()
+
+    launch(x1)
     relay(x0)
-    launch(x1)
+    prepare(x1)
+    compute(x1, 3, 0)
+    relay(x1)
+    gathered(0)
+    cross(z0)
     cross(x0)
-    for job in (z0, z1, x1):
-        prepare(job)
-        relay(job)
-    for job in (z0, z1, x1):
-        compute(job, 3, 0)
+    gathered(1)
+    cross(z1)
     swap(0)
-    for job in (z0, x1, z1):
-        cross(job)
+    cross(x1)
     gx_out[:, :PIECE] = total_of(z0)
     swap(1)
     gx_out[:, PIECE:] = total_of(z1)
     for copy in lasts:
         copy.wait()
-
-
-def finish(dq, dkv, own, turned, wq, wk, wv, cos, sin):
+    for piece in range(2):
+        for copy in spread[piece]:
+            copy.wait_send()
+
+
+def finish(dq, dkv, own, turned, wq, w_all, cos, sin):
     vmem = pl.BlockSpec(memory_space=pltpu.VMEM)
     hbm = pl.BlockSpec(memory_space=pltpu.HBM)
     any_space = pl.BlockSpec(memory_space=pl.ANY)
@@ -700,14 +764,17 @@
             jax.ShapeDtypeStruct((HALF, TOK), BF),
             jax.ShapeDtypeStruct((2, 2, QTR, PIECE), BF),
         ),
-        in_specs=[any_space] * 3 + [hbm] * 4 + [vmem, vmem],
+        in_specs=[any_space] * 3 + [hbm] * 3 + [vmem, vmem],
         out_specs=(vmem,) * 2,
         scratch_shapes=[
             pltpu.VMEM((2, 2, TOK, HD), F32),
             pltpu.VMEM((D, 2 * TOK), BF),
-            pltpu.VMEM((D, 8 * HD), BF),
+            pltpu.VMEM((D, 4 * HD), BF),
+            pltpu.VMEM((4, CHUNK, 4 * HD), BF),
             pltpu.VMEM((4 * HD, 2 * TOK), BF),
-            pltpu.VMEM((8 * HD, TOK), BF),
+            pltpu.VMEM((4 * HD, TOK), BF),
+            pltpu.VMEM((2, 2, 2 * HD, PIECE), BF),
+            pltpu.VMEM((4, 2, 2, 2 * HD, PIECE), BF),
             pltpu.VMEM((2, 2, 2, TOK, HD), BF),
             pltpu.VMEM((2, 2, 2, TOK, HD), BF),
             pltpu.VMEM((2, 2, TOK, HD), BF),
@@ -719,14 +786,14 @@
             pltpu.VMEM((2, 3, HALF, PIECE), BF),
             pltpu.VMEM((2, 3, HALF, PIECE), BF),
             pltpu.VMEM((2, HALF, PIECE), BF),
-            dma((10,)), dma((3,)), dma((2, 2)), dma((2, 2, 2)), dma((2, 2, 2)),
-            dma((2, 2, 4)), dma((2, 2, 4)), dma((2, 2, 2)), dma((2, 2)),
+            dma((16,)), dma((3,)), dma((2, 2)), dma((2, 2, 2)), dma((2, 2, 2)),
+            dma((2, 2, 4)), dma((2, 2, 4)), dma((2, 2, 2)), dma((2, 2)), dma((3, 2, 2)), dma((3, 2, 2)),
         ],
         compiler_params=pltpu.CompilerParams(
             collective_id=1, has_side_effects=True, vmem_limit_bytes=58 << 20
         ),
         name="finish",
-    )(dq, dkv, own, turned, wq, wk, wv, cos, sin)
+    )(dq, dkv, own, turned, wq, w_all, cos, sin)
 
 
 def emit_kernel(gx, gw, gx_out, gq_out, gk_out, gv_out):
@@ -760,9 +827,9 @@
     angles = slots * inverse_freq[None, :, None]
     cos, sin = jnp.cos(angles), jnp.sin(angles)
     base = (2 * chip - 8).astype(jnp.int32).reshape(1)
-    qg, kv, turned = gather(queries, keys, values, out_grad, normed)
+    qg, kv, turned, w_all = gather(queries, keys, values, out_grad, normed, w_key, w_value)
     dq, dkv, own = attend(valid_len, base, qg, kv, cos, sin)
-    gx, gq, gk, gv = emit(*finish(dq, dkv, own, turned, w_query, w_key, w_value, cos, sin))
+    gx, gq, gk, gv = emit(*finish(dq, dkv, own, turned, w_query, w_all, cos, sin))
     return gx.T, gq, gk, gv
 
 

time: 181 us -> 187 us (1.033); the launches traced: 179 us -> 186 us
  Pallas kernels: 176 us -> 184 us
    pallas_call x1, Pallas kernels: 40.2 us -> 44.1 us  [gather(): pl.pallas_call(gather_kernel, out_shape=(jax.ShapeDtypeStruct((2, 2, TOK,...]
    pallas_call x1, Pallas kernels: 109 us -> 112 us  [finish(): pl.pallas_call(finish_kernel, out_shape=(jax.ShapeDtypeStruct((HALF, TOK)...]
where the time goes in v4:
time: 187 us; the launch traced here: 186 us
  Pallas kernels  184 us (98%)
    pallas_call x1, Pallas kernels, finish(): pl.pallas_call(finish_kernel, out_shape=(jax.ShapeDtypeStruct((HALF, TOK)...  112 us
    pallas_call x1, Pallas kernels, gather(): pl.pallas_call(gather_kernel, out_shape=(jax.ShapeDtypeStruct((2, 2, TOK,...  44.1 us
    pallas_call x1, Pallas kernels, attend(): pl.pallas_call(attend_kernel, out_shape=(jax.ShapeDtypeStruct((2, 2 * HD,...  25 us

profile of v4, /device:TPU:1, one launch (start us, length us, event | category | flops | bytes accessed | tf_op | source)
XLA Modules:
  0.0 186.4 jit_solution(12196897352451614171)
XLA Ops:
  0.7 1.8 multiply_sine_fusion
  2.5 44.1 %gather.1 = (bf16[2,2,512,256]{3,2,1,0:T(8,128)(2,1)}, bf16[10,2,512,128]{3,2,1,0:T(8,128)(2,1)}, bf16[2,4608,512]{2,1,0:T(8,128)(2,1)}, bf16[4,2,1152,256]{3,2,1,0:T(8,128)(2,1)}) custom-call(bf16[512,512]{1,0:T(8,128)(2,1)} %q.1, bf16[512,512]{1,0:T(8,128)(2,1)} %g.1, bf16[512,256]{1,0:T(8,128)(2,1)} %k.1, bf16[512,256]{1,0:T(8,128)(2,1)} %v.1, ...), custom_call_target="tpu_custom_call" | custom-call | tf_op jit(solution)/shard_map/gather/pallas_call | solution.py:213
  46.6 25.0 %attend.1 = (bf16[2,256,512]{2,1,0:T(8,128)(2,1)}, bf16[8,2,512,128]{3,2,1,0:T(8,128)(2,1)}, f32[2,2,512,128]{3,2,1,0:T(8,128)}) custom-call(s32[16]{0:T(128)} %valid.1, s32[1]{0:T(128)} %bitcast.base, bf16[2,2,512,256]{3,2,1,0:T(8,128)(2,1)} %get-tuple-element.17.qg, bf16[10,2,4,128,128]{4,3,2,1,0:T(8,128)(2,1)} %bitcast.3, ...), custom_call_target="tpu_custom_call" | custom-call | tf_op jit(solution)/shard_map/attend/pallas_call | solution.py:438
  71.7 112.5 %finish.1 = (bf16[576,512]{1,0:T(8,128)(2,1)}, bf16[2,2,288,256]{3,2,1,0:T(8,128)(2,1)}) custom-call(bf16[2,256,512]{2,1,0:T(8,128)(2,1)} %get-tuple-element.19.dq, bf16[8,2,512,128]{3,2,1,0:T(8,128)(2,1)} %get-tuple-element.20.dkv, f32[2,2,512,128]{3,2,1,0:T(8,128)} %get-tuple-element.21.own_hbm, bf16[2,4608,512]{2,1,0:T(8,128)(2,1)} %get-tuple-element.22.turned_hbm, ...), custom_call_target="tpu_custom_call" | custom-call | tf_op jit(solution)/shard_map/finish/pallas_call | solution.py:761
  184.2 2.3 %emit.1 = (bf16[576,512]{1,0:T(8,128)(2,1)}, bf16[288,512]{1,0:T(8,128)(2,1)}, bf16[288,256]{1,0:T(8,128)(2,1)}, bf16[288,256]{1,0:T(8,128)(2,1)}) custom-call(bf16[576,512]{1,0:T(8,128)(2,1)} %get-tuple-element.24.gx, bf16[2,2,288,256]{3,2,1,0:T(8,128)(2,1)} %get-tuple-element.25.gw), custom_call_target="tpu_custom_call" | custom-call | tf_op jit(solution)/shard_map/emit/pallas_call | solution.py:809
  (2 shorter events, 0.0 us)

commit v5 on v4

--- a/solution.py
+++ b/solution.py
@@ -69,11 +69,11 @@
 
 
 def gather_kernel(
-    q, g, k, v, n_hbm, wk, wv, qg, kv, nt_out, w_all, kv_own, qg_own, n_ref, turned,
+    q, g, k, v, n_hbm, qg, kv, nt_out, kv_own, qg_own, n_ref, turned,
     n_load_sem, kv_load, qg_load, kv_loc, qg_loc, swap_send, swap_recv,
-    x_send, x_recv, y_send, y_recv, n_sem, n_send, n_recv, w_loc, w_send, w_recv, w_pass, w_get,
+    x_send, x_recv, y_send, y_recv, n_sem, n_send, n_recv,
 ):
-    x, yh, core, z, yl = here()
+    x, yh, core, _, _ = here()
     other = 1 - core
     partner = at_seq(x, yh, other)
     across = at_seq(x, 1 - yh, core)
@@ -95,7 +95,6 @@
     greet(
         [partner, across]
         + [at_seq(x + step, yh, c) for step in (1, -1, 2) for c in range(2)]
-        + [at_head(z + step, yl) for step in STEPS]
     )
     for copy in kv_stage:
         copy.wait()
@@ -148,20 +147,6 @@
         for copy in first:
             copy.start()
 
-    part = pl.ds(pl.multiple_of(core * HALF, HALF), HALF)
-    w_keep, w_out, w_on = [], [], []
-    for kind, ref in enumerate((wk, wv)):
-        own_rows = pl.ds(pl.multiple_of(z * CHUNK, CHUNK), CHUNK)
-        w_keep.append(pltpu.make_async_copy(ref.at[own_rows], w_all.at[z, kind], w_loc.at[kind]))
-        for i, step in enumerate(STEPS):
-            rows = pl.ds(pl.multiple_of(lax.rem(z + 4 + step, 4) * CHUNK + core * HALF, HALF), HALF)
-            w_out.append(
-                remote(ref.at[rows], w_all.at[z, kind, part], w_send.at[kind, i], w_recv.at[kind, i], at_head(z + step, yl))
-            )
-            come = w_all.at[lax.rem(z + 4 - step, 4), kind, part]
-            w_on.append(remote(come, come, w_pass.at[kind, i], w_get.at[kind, i], partner))
-    for copy in w_out + w_keep:
-        copy.start()
     for copy in qg_stage:
         copy.wait()
     qg_swap.start()
@@ -191,23 +176,18 @@
         def _():
             second[c].start()
 
-    for out, on in zip(w_out, w_on):
-        out.wait()
-        on.start()
     n_local.wait()
     n_swap.wait()
     qg_keep.wait()
     qg_swap.wait()
     for copy in first + second:
         copy.wait()
-    for copy in w_on + w_keep:
-        copy.wait()
     kv_swap.wait_send()
     for copy in along[0] + along[1]:
         copy.wait_send()
 
 
-def gather(queries, keys, values, grads, normed, wk, wv):
+def gather(queries, keys, values, grads, normed):
     hbm = pl.BlockSpec(memory_space=pltpu.HBM)
     dma = pltpu.SemaphoreType.DMA
     return pl.pallas_call(
@@ -216,10 +196,9 @@
             jax.ShapeDtypeStruct((2, 2, TOK, 2 * HD), BF),
             jax.ShapeDtypeStruct((NB, 2, TOK, HD), BF),
             jax.ShapeDtypeStruct((2, D, TOK), BF),
-            jax.ShapeDtypeStruct((4, 2, CHUNK, 2 * HD), BF),
         ),
-        in_specs=[hbm] * 7,
-        out_specs=(hbm,) * 4,
+        in_specs=[hbm] * 5,
+        out_specs=(hbm,) * 3,
         scratch_shapes=[
             pltpu.VMEM((2, 2, TOK, HD), BF),
             pltpu.VMEM((2, 2, TOK, 2 * HD), BF),
@@ -227,13 +206,12 @@
             pltpu.VMEM((D, TOK), BF),
             dma, dma((2, 2)), dma((2, 2)), dma, dma, dma((2,)), dma((2,)),
             dma((2, 2)), dma((2, 2)), dma((2, 2)), dma((2, 2)), dma, dma, dma,
-            dma((2,)), dma((2, 3)), dma((2, 3)), dma((2, 3)), dma((2, 3)),
         ],
         compiler_params=pltpu.CompilerParams(
             collective_id=0, has_side_effects=True, vmem_limit_bytes=60 << 20
         ),
         name="gather",
-    )(queries, grads, keys, values, normed, wk, wv)
+    )(queries, grads, keys, values, normed)
 
 
 STEP = 8
@@ -458,6 +436,7 @@
             pltpu.SemaphoreType.DMA,
         ],
         compiler_params=pltpu.CompilerParams(vmem_limit_bytes=58 << 20),
+        cost_estimate=pl.CostEstimate(flops=26_000_000_000, bytes_accessed=8 << 20, transcendentals=20_000_000),
         name="attend",
     )(valid_len, base, qg, kv.reshape(NB, 2, 4, HD, HD), cos, sin)
 
@@ -466,10 +445,11 @@
 
 
 def finish_kernel(
-    dq, dkv, own_hbm, turned_hbm, wq, w_all, cos, sin, gx_out, gw_out,
-    own, n_buf, w_buf, wkv_buf, t_buf, d_buf, dkv_t, g_buf, y_buf, x_buf, near, far,
-    xs, xr, zs, zr, xy, zy, half_buf,
+    dq, dkv, own_hbm, turned_hbm, wq, wk, wv, w_near, w_back, w_far, cos, sin, gx_out, gw_out,
+    own, n_buf, w_buf, t_buf, dkv_t, gq_buf, g_buf, zq_buf, y_buf, x_buf, near, far,
+    xs, xr, xy, zy, half_buf,
     load_sem, dq_sems, dk_sems, y_sems, x_sems, ring_send, ring_recv, pair_sems, core_sems, g_send, g_recv,
+    gq_send, gq_recv, w_load, w_send, w_recv,
 ):
     x, yh, core, z, yl = here()
     other = 1 - core
@@ -477,7 +457,6 @@
     across = at_seq(x, 1 - yh, core)
     beside = at_head(z, 1 - yl)
     x_next, x_prev, x_far = at_seq(x + 1, yh, core), at_seq(x - 1, yh, core), at_seq(x + 2, yh, core)
-    z_next, z_prev = at_head(z + 1, yl), at_head(z - 1, yl)
     round_z = [[at_core(z + step, yl, c) for c in range(2)] for step in STEPS]
     greet([partner, across, beside, x_next, x_prev, x_far] + sum(round_z, []))
 
@@ -493,23 +472,37 @@
     pairs = [
         (dkv.at[pl.ds(0, 2)], far),
         (dkv.at[pl.ds(4, 2)], near),
-        (wq, w_buf),
         (dq.at[0], t_buf.at[: 2 * HD, :TOK]),
         (dq.at[1], t_buf.at[: 2 * HD, TOK:]),
         (turned_hbm.at[0], n_buf.at[:, :TOK]),
         (turned_hbm.at[1], n_buf.at[:, TOK:]),
         (own_hbm, own),
-    ] + [
-        (w_all.at[i, kind], wkv_buf.at[i, :, kind * 2 * HD : (kind + 1) * 2 * HD])
-        for i in range(4)
-        for kind in range(2)
     ]
     loads = [pltpu.make_async_copy(src, dst, load_sem.at[i]) for i, (src, dst) in enumerate(pairs)]
     for copy in loads:
         copy.start()
-    head_rows = pl.ds(pl.multiple_of(core * 2 * HD, 2 * HD), 2 * HD)
-    dq_swap = remote(dq.at[other], d_buf.at[head_rows], dq_sems.at[0], dq_sems.at[1], partner)
-    dq_keep = pltpu.make_async_copy(dq.at[core], d_buf.at[head_rows], dq_sems.at[2])
+    q_spread = [
+        remote(dq.at[r], gq_buf.at[i, core], gq_send.at[i, r], gq_recv.at[i, core], round_z[i][r])
+        for i in range(3)
+        for r in range(2)
+    ]
+    q_kin = remote(dq.at[other], gq_buf.at[3, core], dq_sems.at[0], dq_sems.at[1], partner)
+    q_keep = pltpu.make_async_copy(dq.at[core], gq_buf.at[3, core], dq_sems.at[2])
+    part = pl.ds(pl.multiple_of(core * HALF, HALF), HALF)
+    own_rows = pl.ds(pl.multiple_of(z * CHUNK, CHUNK), CHUNK)
+    w_in = [
+        pltpu.make_async_copy(src, w_buf.at[i, part], w_load.at[i])
+        for i, src in enumerate((w_near, w_back, w_far))
+    ] + [
+        pltpu.make_async_copy(ref.at[own_rows], w_buf.at[3, :, cols], w_load.at[3 + i])
+        for i, (ref, cols) in enumerate(
+            ((wq, slice(0, 4 * HD)), (wk, slice(4 * HD, 6 * HD)), (wv, slice(6 * HD, 8 * HD)))
+        )
+    ]
+    w_on = [
+        remote(src, w_buf.at[i, part], w_send.at[i], w_recv.at[i], partner)
+        for i, src in enumerate((w_near, w_back, w_far))
+    ]
     back_near, back_far = (
         [
             remote(src.at[r], x_buf.at[i, r], x_sems.at[0, i, r], x_sems.at[1, i, r], device)
@@ -524,72 +517,58 @@
         for copy in back_far:
             copy.start()
 
-    dq_swap.start()
-    dq_keep.start()
-    for copy in loads[1:3]:
+    for copy in q_spread + [q_kin, q_keep] + w_on + w_in:
+        copy.start()
+    for copy in loads[1:]:
         copy.wait()
-    dq_keep.wait()
-    dq_swap.wait()
-
-    send, recv = (xs, zs), (xr, zr)
-    ahead, behind = (x_next, z_next), (x_prev, z_prev)
-    place = (x, z)
-
-    def term(axis, piece, rows):
-        part = slice(piece * PIECE, (piece + 1) * PIECE)
-        if axis == 0:
-            return nt(n_buf[rows, :], t_buf[part, :])
-        return nn(w_buf[rows, :], d_buf[:, part])
-
-    def compute(job, slot, step):
-        axis, piece = job
-        first_row = lax.rem(place[axis] + step, 4) * CHUNK
+
+    def term(piece, rows):
+        return nt(n_buf[rows, :], t_buf[piece * PIECE : (piece + 1) * PIECE, :])
+
+    def compute(piece, slot, step):
+        first_row = lax.rem(x + step, 4) * CHUNK
 
         def one(half, carry):
             to = pl.ds(pl.multiple_of(half * HALF, HALF), HALF)
             rows = pl.ds(pl.multiple_of(first_row + half * HALF, HALF), HALF)
-            send[axis][piece, slot, to, :] = term(axis, piece, rows).astype(BF)
+            xs[piece, slot, to, :] = term(piece, rows).astype(BF)
             return carry
 
         lax.fori_loop(0, 2, one, 0)
 
-    def ring(job):
-        axis, piece = job
-        out, come = send[axis].at[piece], recv[axis].at[piece]
+    def ring(piece):
+        out, come = xs.at[piece], xr.at[piece]
         top, low = pl.ds(0, HALF), pl.ds(HALF, HALF)
         spans = (
-            (out.at[0, top], come.at[0, top], ahead[axis]),
-            (out.at[0, low], come.at[0, low], behind[axis]),
-            (out.at[1], come.at[1], ahead[axis]),
-            (out.at[2], come.at[2], behind[axis]),
+            (out.at[0, top], come.at[0, top], x_next),
+            (out.at[0, low], come.at[0, low], x_prev),
+            (out.at[1], come.at[1], x_next),
+            (out.at[2], come.at[2], x_prev),
         )
         return [
-            remote(src, dst, ring_send.at[axis, piece, i], ring_recv.at[axis, piece, i], device)
+            remote(src, dst, ring_send.at[piece, i], ring_recv.at[piece, i], device)
             for i, (src, dst, device) in enumerate(spans)
         ]
 
+    rings = [ring(piece) for piece in range(2)]
+
+    def launch(piece):
+        compute(piece, 0, 2)
+        rings[piece][0].start()
+        rings[piece][1].start()
+
+    def prepare(piece):
+        compute(piece, 1, 1)
+        compute(piece, 2, 3)
+
+    def relay(piece):
+        for way, rows in ((0, slice(0, HALF)), (1, slice(HALF, CHUNK))):
+            rings[piece][way].wait()
+            mine = xs[piece, 1 + way, rows, :].astype(F32)
+            xs[piece, 1 + way, rows, :] = (mine + xr[piece, 0, rows, :].astype(F32)).astype(BF)
+            rings[piece][2 + way].start()
+
     x0, x1, z0, z1 = jobs = ((0, 0), (0, 1), (1, 0), (1, 1))
-    rings = {job: ring(job) for job in jobs}
-
-    def launch(job):
-        compute(job, 0, 2)
-        rings[job][0].start()
-        rings[job][1].start()
-
-    def prepare(job):
-        compute(job, 1, 1)
-        compute(job, 2, 3)
-
-    def relay(job):
-        axis, piece = job
-        for way, rows in ((0, slice(0, HALF)), (1, slice(HALF, CHUNK))):
-            rings[job][way].wait()
-            mine = send[axis][piece, 1 + way, rows, :].astype(F32)
-            send[axis][piece, 1 + way, rows, :] = (
-                mine + recv[axis][piece, 0, rows, :].astype(F32)
-            ).astype(BF)
-            rings[job][2 + way].start()
-
     side, side_device, pair_buf = (yh, yl), (across, beside), (xy, zy)
 
     def pair(job):
@@ -601,30 +580,41 @@
 
     pairs_of = {job: pair(job) for job in jobs}
 
+    def queries_part(half, carry):
+        rows = pl.ds(pl.multiple_of(half * HALF, HALF), HALF)
+        for piece in range(2):
+            cols = slice(piece * PIECE, (piece + 1) * PIECE)
+            total = jnp.zeros((HALF, PIECE), F32)
+            for i in range(4):
+                found = jnp.concatenate([gq_buf[i, head, :, cols] for head in range(2)], axis=0)
+                total += nn(w_buf[i, rows, : 4 * HD], found)
+            zq_buf[rows, cols] = total
+        return carry
+
     def keys_part(piece, rows):
-        total = jnp.zeros((HALF, PIECE), F32)
+        total = zq_buf[rows, piece * PIECE : (piece + 1) * PIECE]
         for i in range(4):
             found = [
                 g_buf[i, head, piece, kind * HD : (kind + 1) * HD, :] for kind in range(2) for head in range(2)
             ]
-            total += nn(wkv_buf[i, rows, :], jnp.concatenate(found, axis=0))
+            total += nn(w_buf[i, rows, 4 * HD :], jnp.concatenate(found, axis=0))
         return total
 
     def cross(job):
         axis, piece = job
-        rings[job][2].wait()
-        rings[job][3].wait()
+        if axis == 0:
+            rings[piece][2].wait()
+            rings[piece][3].wait()
 
         def summed(half):
             rows = pl.ds(pl.multiple_of(half * HALF, HALF), HALF)
-            total = (
-                send[axis][piece, 3, rows, :].astype(F32)
-                + recv[axis][piece, 1, rows, :].astype(F32)
-                + recv[axis][piece, 2, rows, :].astype(F32)
-            )
             if axis == 1:
-                total += keys_part(piece, rows)
-            return total.astype(BF)
+                return keys_part(piece, rows).astype(BF)
+            return (
+                xs[piece, 3, rows, :].astype(F32)
+                + xr[piece, 1, rows, :].astype(F32)
+                + xr[piece, 2, rows, :].astype(F32)
+            ).astype(BF)
 
         pair_buf[axis][piece, 0] = summed(1 - side[axis])
         pairs_of[job].start()
@@ -672,22 +662,20 @@
             add_to(near, 0, r)
             back_near[r].start()
 
-    launch(z0)
-    launch(z1)
-    prepare(z0)
-    prepare(z1)
+    launch(0)
+    prepare(0)
+    compute(0, 3, 0)
     for r in range(2):
         further(r)
-    relay(z0)
-    relay(z1)
     for r in range(2):
         nearer(r)
-    for copy in loads[3:]:
+    for copy in w_in + w_on + [q_kin, q_keep]:
         copy.wait()
-    launch(x0)
-    prepare(x0)
-    for job in (z0, z1, x0):
-        compute(job, 3, 0)
+    for i in range(3):
+        for head in range(2):
+            come = gq_buf.at[i, head]
+            remote(come, come, gq_send.at[i, head], gq_recv.at[i, head], partner).wait_recv()
+    lax.fori_loop(0, 2, queries_part, 0)
     keep = (yh == 0).astype(F32)
     for copy in back_far + back_near:
         copy.wait()
@@ -709,33 +697,33 @@
                 dkv_t[r, piece, kind * HD : (kind + 1) * HD, :] = total[:, piece * PIECE : (piece + 1) * PIECE]
     spread = [
         [
-            remote(dkv_t.at[r, piece], g_buf.at[z, core, piece], g_send.at[i, r, piece], g_recv.at[i, core, piece], round_z[i][r])
+            remote(dkv_t.at[r, piece], g_buf.at[i, core, piece], g_send.at[i, r, piece], g_recv.at[i, core, piece], round_z[i][r])
             for i in range(3)
             for r in range(2)
         ]
         for piece in range(2)
     ]
     kin = [
-        remote(dkv_t.at[other, piece], g_buf.at[z, core, piece], dk_sems.at[0, piece], dk_sems.at[1, piece], partner)
+        remote(dkv_t.at[other, piece], g_buf.at[3, core, piece], dk_sems.at[0, piece], dk_sems.at[1, piece], partner)
         for piece in range(2)
     ]
     for piece in range(2):
         for copy in spread[piece] + [kin[piece]]:
             copy.start()
-        g_buf[z, core, piece] = dkv_t[core, piece]
+        g_buf[3, core, piece] = dkv_t[core, piece]
 
     def gathered(piece):
         kin[piece].wait()
-        for i, step in enumerate(STEPS):
+        for i in range(3):
             for head in range(2):
-                come = g_buf.at[lax.rem(z + 4 - step, 4), head, piece]
+                come = g_buf.at[i, head, piece]
                 remote(come, come, g_send.at[i, head, piece], g_recv.at[i, head, piece], partner).wait_recv()
 
-    launch(x1)
-    relay(x0)
-    prepare(x1)
-    compute(x1, 3, 0)
-    relay(x1)
+    launch(1)
+    relay(0)
+    prepare(1)
+    compute(1, 3, 0)
+    relay(1)
     gathered(0)
     cross(z0)
     cross(x0)
@@ -748,12 +736,11 @@
     gx_out[:, PIECE:] = total_of(z1)
     for copy in lasts:
         copy.wait()
-    for piece in range(2):
-        for copy in spread[piece]:
-            copy.wait_send()
-
-
-def finish(dq, dkv, own, turned, wq, w_all, cos, sin):
+    for copy in q_spread + spread[0] + spread[1]:
+        copy.wait_send()
+
+
+def finish(dq, dkv, own, turned, weights, w_rows, cos, sin):
     vmem = pl.BlockSpec(memory_space=pltpu.VMEM)
     hbm = pl.BlockSpec(memory_space=pltpu.HBM)
     any_space = pl.BlockSpec(memory_space=pl.ANY)
@@ -764,36 +751,35 @@
             jax.ShapeDtypeStruct((HALF, TOK), BF),
             jax.ShapeDtypeStruct((2, 2, QTR, PIECE), BF),
         ),
-        in_specs=[any_space] * 3 + [hbm] * 3 + [vmem, vmem],
+        in_specs=[any_space] * 3 + [hbm] * 4 + [any_space] * 3 + [vmem, vmem],
         out_specs=(vmem,) * 2,
         scratch_shapes=[
             pltpu.VMEM((2, 2, TOK, HD), F32),
             pltpu.VMEM((D, 2 * TOK), BF),
-            pltpu.VMEM((D, 4 * HD), BF),
-            pltpu.VMEM((4, CHUNK, 4 * HD), BF),
+            pltpu.VMEM((4, CHUNK, 8 * HD), BF),
             pltpu.VMEM((4 * HD, 2 * TOK), BF),
-            pltpu.VMEM((4 * HD, TOK), BF),
             pltpu.VMEM((2, 2, 2 * HD, PIECE), BF),
+            pltpu.VMEM((4, 2, 2 * HD, TOK), BF),
             pltpu.VMEM((4, 2, 2, 2 * HD, PIECE), BF),
+            pltpu.VMEM((CHUNK, TOK), F32),
             pltpu.VMEM((2, 2, 2, TOK, HD), BF),
             pltpu.VMEM((2, 2, 2, TOK, HD), BF),
             pltpu.VMEM((2, 2, TOK, HD), BF),
             pltpu.VMEM((2, 2, TOK, HD), BF),
             pltpu.VMEM((2, 4, CHUNK, PIECE), BF),
             pltpu.VMEM((2, 3, CHUNK, PIECE), BF),
-            pltpu.VMEM((2, 4, CHUNK, PIECE), BF),
-            pltpu.VMEM((2, 3, CHUNK, PIECE), BF),
             pltpu.VMEM((2, 3, HALF, PIECE), BF),
             pltpu.VMEM((2, 3, HALF, PIECE), BF),
             pltpu.VMEM((2, HALF, PIECE), BF),
-            dma((16,)), dma((3,)), dma((2, 2)), dma((2, 2, 2)), dma((2, 2, 2)),
-            dma((2, 2, 4)), dma((2, 2, 4)), dma((2, 2, 2)), dma((2, 2)), dma((3, 2, 2)), dma((3, 2, 2)),
+            dma((8,)), dma((3,)), dma((2, 2)), dma((2, 2, 2)), dma((2, 2, 2)),
+            dma((2, 4)), dma((2, 4)), dma((2, 2, 2)), dma((2, 2)), dma((3, 2, 2)), dma((3, 2, 2)),
+            dma((3, 2)), dma((3, 2)), dma((6,)), dma((3,)), dma((3,)),
         ],
         compiler_params=pltpu.CompilerParams(
-            collective_id=1, has_side_effects=True, vmem_limit_bytes=58 << 20
+            collective_id=1, has_side_effects=True, vmem_limit_bytes=54 << 20
         ),
         name="finish",
-    )(dq, dkv, own, turned, wq, w_all, cos, sin)
+    )(dq, dkv, own, turned, *weights, *w_rows, cos, sin)
 
 
 def emit_kernel(gx, gw, gx_out, gq_out, gk_out, gv_out):
@@ -827,9 +813,17 @@
     angles = slots * inverse_freq[None, :, None]
     cos, sin = jnp.cos(angles), jnp.sin(angles)
     base = (2 * chip - 8).astype(jnp.int32).reshape(1)
-    qg, kv, turned, w_all = gather(queries, keys, values, out_grad, normed, w_key, w_value)
+    core, z = lax.axis_index("seq") % 2, lax.axis_index("head") // 2
+    weights = (w_query, w_key, w_value)
+    w_rows = []
+    for step in STEPS:
+        start = ((z + 4 + step) % 4) * CHUNK + core * HALF
+        rows = jnp.concatenate([lax.dynamic_slice_in_dim(w, start, HALF, 0) for w in weights], axis=1)
+        turns = [(h, (h + 2 * step) % 8) for h in range(8)]
+        w_rows.append(lax.ppermute(rows, "head", turns))
+    qg, kv, turned = gather(queries, keys, values, out_grad, normed)
     dq, dkv, own = attend(valid_len, base, qg, kv, cos, sin)
-    gx, gq, gk, gv = emit(*finish(dq, dkv, own, turned, w_query, w_all, cos, sin))
+    gx, gq, gk, gv = emit(*finish(dq, dkv, own, turned, weights, w_rows, cos, sin))
     return gx.T, gq, gk, gv
 
 

time: 187 us -> 190 us (1.016)
  Pallas kernels: 184 us -> 173 us
  starting transfers between devices: 0 us -> 5.89 us
  local copies, waits for them, and re-layouts: 0 us -> 4.79 us
  other arithmetic: 1.83 us -> 5.42 us
    pallas_call x1, Pallas kernels: 25 us -> 15.8 us  [attend(): pl.pallas_call(attend_kernel, out_shape=(jax.ShapeDtypeStruct((2, 2 * HD,...]
    ppermute x0 -> x3, starting transfers between devices: none -> 5.89 us  [body(): w_rows.append(lax.ppermute(rows, 'head', turns))]
    pallas_call x1, Pallas kernels: 44.1 us -> 40.4 us  [gather(): pl.pallas_call(gather_kernel, out_shape=(jax.ShapeDtypeStruct((2, 2, TOK,...]
    concatenate x0 -> x3, other arithmetic: none -> 3.6 us  [body(): jnp.concatenate([lax.dynamic_slice_in_dim(w, start, HALF, 0) for w in wei...]
    dynamic_slice x0 -> x2, local copies, waits for them, and re-layouts: none -> 3.08 us  [body(): lax.dynamic_slice_in_dim(w, start, HALF, 0)]
    pallas_call x1, Pallas kernels: 112 us -> 115 us  [finish(): pl.pallas_call(finish_kernel, out_shape=(jax.ShapeDtypeStruct((HALF, TOK)...]
  transfers between devices with their start and end apart: 0 -> 3, of which waited for: 0 -> 0; matrix products, arithmetic and copies ran while one was open for 0% -> 2% of each run, Pallas kernels for 0% -> 30%
where the time goes in v5:
time: 190 us
  Pallas kernels  173 us (91%)
  starting transfers between devices  5.89 us (3%)
  other arithmetic  5.42 us (3%)
  local copies, waits for them, and re-layouts  4.79 us (3%)
    pallas_call x1, Pallas kernels, finish(): pl.pallas_call(finish_kernel, out_shape=(jax.ShapeDtypeStruct((HALF, TOK)...  115 us
    pallas_call x1, Pallas kernels, gather(): pl.pallas_call(gather_kernel, out_shape=(jax.ShapeDtypeStruct((2, 2, TOK,...  40.4 us
    pallas_call x1, Pallas kernels, attend(): pl.pallas_call(attend_kernel, out_shape=(jax.ShapeDtypeStruct((2, 2 * HD,...  15.8 us
    ppermute x3, starting transfers between devices, body(): w_rows.append(lax.ppermute(rows, 'head', turns))  5.89 us
  transfers between devices with their start and end apart: 3, of which 0 were waited for; matrix products, arithmetic and copies ran while one was open for 2% of the time, Pallas kernels for 30%

profile of v5, /device:TPU:1, one launch (start us, length us, event | category | flops | bytes accessed | tf_op | source)
XLA Modules:
  0.0 190.0 jit_solution(6838374174636549400)
XLA Ops:
  0.7 1.5 constant_dynamic-slice_fusion.2
  2.3 1.5 constant_dynamic-slice_fusion
  3.8 1.2 pad_maximum_fusion
  5.0 2.5 %collective-permute-start = (bf16[576,1024]{1,0:T(8,128)(2,1)}, bf16[576,1024]{1,0:T(8,128)(2,1)S(1)}, u32[]{:S(2)}, u32[]{:S(2)}) collective-permute-start(bf16[576,1024]{1,0:T(8,128)(2,1)} %pad_maximum_fusion), channel_id=1, source_target_pairs={{0,2},{1,3},{2,4},{3,5},{4,6},{5,7},{6,0},{7,1},{8,10},{9,11},{10,... | collective-permute-start | bytes 3538952 | tf_op jit(solution)/shard_map/ppermute | solution.py:823
  7.5 1.2 pad_maximum_fusion.1
  8.7 2.1 %collective-permute-start.1 = (bf16[576,1024]{1,0:T(8,128)(2,1)}, bf16[576,1024]{1,0:T(8,128)(2,1)S(1)}, u32[]{:S(2)}, u32[]{:S(2)}) collective-permute-start(bf16[576,1024]{1,0:T(8,128)(2,1)} %pad_maximum_fusion.1), channel_id=1, source_target_pairs={{0,6},{1,7},{2,0},{3,1},{4,2},{5,3},{6,4},{7,5},{8,14},{9,15},{10,... | collective-permute-start | bytes 3538952 | tf_op jit(solution)/shard_map/ppermute | solution.py:823
  10.8 1.2 pad_maximum_fusion.2
  12.0 1.3 collective-permute-start.2
  13.3 1.8 multiply_sine_fusion
  15.1 40.4 %gather.1 = (bf16[2,2,512,256]{3,2,1,0:T(8,128)(2,1)}, bf16[10,2,512,128]{3,2,1,0:T(8,128)(2,1)}, bf16[2,4608,512]{2,1,0:T(8,128)(2,1)}) custom-call(bf16[512,512]{1,0:T(8,128)(2,1)} %q.1, bf16[512,512]{1,0:T(8,128)(2,1)} %g.1, bf16[512,256]{1,0:T(8,128)(2,1)} %k.1, bf16[512,256]{1,0:T(8,128)(2,1)} %v.1, bf16[512,4608]{1,0:T(8,128)(2,1)} %n_hbm.1), custom_call_target="tpu_custom_call" | custom-call | tf_op jit(solution)/shard_map/gather/pallas_call | solution.py:193
  55.5 15.8 %attend.1 = (bf16[2,256,512]{2,1,0:T(8,128)(2,1)}, bf16[8,2,512,128]{3,2,1,0:T(8,128)(2,1)}, f32[2,2,512,128]{3,2,1,0:T(8,128)}) custom-call(s32[16]{0:T(128)} %valid.1, s32[1]{0:T(128)} %bitcast.base, bf16[2,2,512,256]{3,2,1,0:T(8,128)(2,1)} %get-tuple-element.16.qg, bf16[10,2,4,128,128]{4,3,2,1,0:T(8,128)(2,1)} %bitcast.3, ...), custom_call_target="tpu_custom_call" | custom-call | flops 25999998976 | bytes 8388608 | tf_op jit(solution)/shard_map/attend/pallas_call | solution.py:416
  71.3 0.0 collective-permute-done.w_near
  71.3 0.0 copy-start
  71.3 0.0 collective-permute-done.1.w_back
  71.4 0.0 copy-start.1
  71.4 0.0 collective-permute-done.2.w_far
  71.4 0.0 copy-start.2
  71.4 1.0 copy-done
  72.4 0.4 copy-done.1
  72.7 0.4 copy-done.2
  73.1 114.6 %finish.1 = (bf16[576,512]{1,0:T(8,128)(2,1)}, bf16[2,2,288,256]{3,2,1,0:T(8,128)(2,1)}) custom-call(bf16[2,256,512]{2,1,0:T(8,128)(2,1)} %get-tuple-element.18.dq, bf16[8,2,512,128]{3,2,1,0:T(8,128)(2,1)} %get-tuple-element.19.dkv, f32[2,2,512,128]{3,2,1,0:T(8,128)} %get-tuple-element.20.own_hbm, bf16[2,4608,512]{2,1,0:T(8,128)(2,1)} %get-tuple-element.21.turned_hbm, ...), custom_call_target="tpu_custom_call" | custom-call | tf_op jit(solution)/shard_map/finish/pallas_call | solution.py:748
  187.7 2.3 %emit.1 = (bf16[576,512]{1,0:T(8,128)(2,1)}, bf16[288,512]{1,0:T(8,128)(2,1)}, bf16[288,256]{1,0:T(8,128)(2,1)}, bf16[288,256]{1,0:T(8,128)(2,1)}) custom-call(bf16[576,512]{1,0:T(8,128)(2,1)} %get-tuple-element.22.gx, bf16[2,2,288,256]{3,2,1,0:T(8,128)(2,1)} %get-tuple-element.23.gw), custom_call_target="tpu_custom_call" | custom-call | tf_op jit(solution)/shard_map/emit/pallas_call | solution.py:795
  (2 shorter events, 0.0 us)
Async XLA Ops:
  5.0 66.3 %collective-permute-start = (bf16[576,1024]{1,0:T(8,128)(2,1)}, bf16[576,1024]{1,0:T(8,128)(2,1)S(1)}, u32[]{:S(2)}, u32[]{:S(2)}) collective-permute-start(bf16[576,1024]{1,0:T(8,128)(2,1)} %pad_maximum_fusion), channel_id=1, source_target_pairs={{0,2},{1,3},{2,4},{3,5},{4,6},{5,7},{6,0},{7,1},{8,10},{9,11},{10,... | collective-permute-start | bytes 3538952 | tf_op jit(solution)/shard_map/ppermute | solution.py:823
  8.7 62.7 %collective-permute-start.1 = (bf16[576,1024]{1,0:T(8,128)(2,1)}, bf16[576,1024]{1,0:T(8,128)(2,1)S(1)}, u32[]{:S(2)}, u32[]{:S(2)}) collective-permute-start(bf16[576,1024]{1,0:T(8,128)(2,1)} %pad_maximum_fusion.1), channel_id=1, source_target_pairs={{0,6},{1,7},{2,0},{3,1},{4,2},{5,3},{6,4},{7,5},{8,14},{9,15},{10,... | collective-permute-start | bytes 3538952 | tf_op jit(solution)/shard_map/ppermute | solution.py:823
  12.0 59.4 %collective-permute-start.2 = (bf16[576,1024]{1,0:T(8,128)(2,1)}, bf16[576,1024]{1,0:T(8,128)(2,1)S(1)}, u32[]{:S(2)}, u32[]{:S(2)}) collective-permute-start(bf16[576,1024]{1,0:T(8,128)(2,1)} %pad_maximum_fusion.2), channel_id=1, source_target_pairs={{0,4},{1,5},{2,6},{3,7},{4,0},{5,1},{6,2},{7,3},{8,12},{9,13},{10,... | collective-permute-start | bytes 3538952 | tf_op jit(solution)/shard_map/ppermute | solution.py:823
  71.3 1.0 copy-start
  71.4 1.4 copy-start.1
  71.4 1.7 copy-start.2

commit v6 on v5

--- a/solution.py
+++ b/solution.py
@@ -66,6 +66,32 @@
     for device in devices:
         pl.semaphore_signal(barrier, inc=1, device_id=device, device_id_type=MESH)
     pl.semaphore_wait(barrier, len(devices))
+
+
+def pack_kernel(wq, wk, wv, out, sem):
+    _, _, core, _, _ = here()
+    copies = []
+    for i in range(4):
+        rows = pl.ds(pl.multiple_of(i * CHUNK + core * HALF, HALF), HALF)
+        for j, (ref, first, last) in enumerate(((wq, 0, 4), (wk, 4, 6), (wv, 6, 8))):
+            to = out.at[i, :, first * HD : last * HD]
+            copies.append(pltpu.make_async_copy(ref.at[rows], to, sem.at[i, j]))
+    for copy in copies:
+        copy.start()
+    for copy in copies:
+        copy.wait()
+
+
+def pack(weights):
+    hbm = pl.BlockSpec(memory_space=pltpu.HBM)
+    return pl.pallas_call(
+        pack_kernel,
+        out_shape=jax.ShapeDtypeStruct((4, HALF, 8 * HD), BF),
+        in_specs=[hbm] * 3,
+        out_specs=hbm,
+        scratch_shapes=[pltpu.SemaphoreType.DMA((4, 3))],
+        name="pack",
+    )(*weights)
 
 
 def gather_kernel(
@@ -445,7 +471,7 @@
 
 
 def finish_kernel(
-    dq, dkv, own_hbm, turned_hbm, wq, wk, wv, w_near, w_back, w_far, cos, sin, gx_out, gw_out,
+    dq, dkv, own_hbm, turned_hbm, wq, wk, wv, w_rows, cos, sin, gx_out, gw_out,
     own, n_buf, w_buf, t_buf, dkv_t, gq_buf, g_buf, zq_buf, y_buf, x_buf, near, far,
     xs, xr, xy, zy, half_buf,
     load_sem, dq_sems, dk_sems, y_sems, x_sems, ring_send, ring_recv, pair_sems, core_sems, g_send, g_recv,
@@ -490,9 +516,10 @@
     q_keep = pltpu.make_async_copy(dq.at[core], gq_buf.at[3, core], dq_sems.at[2])
     part = pl.ds(pl.multiple_of(core * HALF, HALF), HALF)
     own_rows = pl.ds(pl.multiple_of(z * CHUNK, CHUNK), CHUNK)
+    w_from = [w_rows.at[lax.rem(z + 4 - step, 4)] for step in STEPS]
     w_in = [
         pltpu.make_async_copy(src, w_buf.at[i, part], w_load.at[i])
-        for i, src in enumerate((w_near, w_back, w_far))
+        for i, src in enumerate(w_from)
     ] + [
         pltpu.make_async_copy(ref.at[own_rows], w_buf.at[3, :, cols], w_load.at[3 + i])
         for i, (ref, cols) in enumerate(
@@ -501,7 +528,7 @@
     ]
     w_on = [
         remote(src, w_buf.at[i, part], w_send.at[i], w_recv.at[i], partner)
-        for i, src in enumerate((w_near, w_back, w_far))
+        for i, src in enumerate(w_from)
     ]
     back_near, back_far = (
         [
@@ -751,7 +778,7 @@
             jax.ShapeDtypeStruct((HALF, TOK), BF),
             jax.ShapeDtypeStruct((2, 2, QTR, PIECE), BF),
         ),
-        in_specs=[any_space] * 3 + [hbm] * 4 + [any_space] * 3 + [vmem, vmem],
+        in_specs=[any_space] * 3 + [hbm] * 5 + [vmem, vmem],
         out_specs=(vmem,) * 2,
         scratch_shapes=[
             pltpu.VMEM((2, 2, TOK, HD), F32),
@@ -779,7 +806,7 @@
             collective_id=1, has_side_effects=True, vmem_limit_bytes=54 << 20
         ),
         name="finish",
-    )(dq, dkv, own, turned, *weights, *w_rows, cos, sin)
+    )(dq, dkv, own, turned, *weights, w_rows, cos, sin)
 
 
 def emit_kernel(gx, gw, gx_out, gq_out, gk_out, gv_out):
@@ -813,14 +840,9 @@
     angles = slots * inverse_freq[None, :, None]
     cos, sin = jnp.cos(angles), jnp.sin(angles)
     base = (2 * chip - 8).astype(jnp.int32).reshape(1)
-    core, z = lax.axis_index("seq") % 2, lax.axis_index("head") // 2
     weights = (w_query, w_key, w_value)
-    w_rows = []
-    for step in STEPS:
-        start = ((z + 4 + step) % 4) * CHUNK + core * HALF
-        rows = jnp.concatenate([lax.dynamic_slice_in_dim(w, start, HALF, 0) for w in weights], axis=1)
-        turns = [(h, (h + 2 * step) % 8) for h in range(8)]
-        w_rows.append(lax.ppermute(rows, "head", turns))
+    lines = [[2 * z + yl for z in range(4)] for yl in range(2)]
+    w_rows = lax.all_to_all(pack(weights), "head", 0, 0, axis_index_groups=lines, tiled=True)
     qg, kv, turned = gather(queries, keys, values, out_grad, normed)
     dq, dkv, own = attend(valid_len, base, qg, kv, cos, sin)
     gx, gq, gk, gv = emit(*finish(dq, dkv, own, turned, weights, w_rows, cos, sin))

time: 190 us -> 320 us (1.68)
  Pallas kernels: 173 us -> 312 us
  local copies, waits for them, and re-layouts: 4.79 us -> 0 us
  other arithmetic: 5.42 us -> 1.84 us
    pallas_call x0 -> x1, Pallas kernels: none -> 144 us  [pack(): pl.pallas_call(pack_kernel, out_shape=jax.ShapeDtypeStruct((4, HALF, 8 *...]
    pallas_call x1, Pallas kernels: 115 us -> 100 us  [finish(): pl.pallas_call(finish_kernel, out_shape=(jax.ShapeDtypeStruct((HALF, TOK)...]
    pallas_call x1, Pallas kernels: 15.8 us -> 25 us  [attend(): pl.pallas_call(attend_kernel, out_shape=(jax.ShapeDtypeStruct((2, 2 * HD,...]
    ppermute x3 -> x0, starting transfers between devices: 5.89 us -> none  [body(): w_rows.append(lax.ppermute(rows, 'head', turns))]
    all_to_all x0 -> x1, starting transfers between devices: none -> 5.87 us  [body(): lax.all_to_all(pack(weights), 'head', 0, 0, axis_index_groups=lines, tile...]
    concatenate x3 -> x0, other arithmetic: 3.6 us -> none  [body(): jnp.concatenate([lax.dynamic_slice_in_dim(w, start, HALF, 0) for w in wei...]
  transfers between devices with their start and end apart: 3 -> 1, of which waited for: 0 -> 0; matrix products, arithmetic and copies ran while one was open for 2% -> 1% of each run, Pallas kernels for 30% -> 20%
where the time goes in v6:
time: 320 us
  Pallas kernels  312 us (98%)
  starting transfers between devices  5.87 us (2%)
    pallas_call x1, Pallas kernels, pack(): pl.pallas_call(pack_kernel, out_shape=jax.ShapeDtypeStruct((4, HALF, 8 *...  144 us
    pallas_call x1, Pallas kernels, finish(): pl.pallas_call(finish_kernel, out_shape=(jax.ShapeDtypeStruct((HALF, TOK)...  100 us
    pallas_call x1, Pallas kernels, gather(): pl.pallas_call(gather_kernel, out_shape=(jax.ShapeDtypeStruct((2, 2, TOK,...  39.9 us
    pallas_call x1, Pallas kernels, attend(): pl.pallas_call(attend_kernel, out_shape=(jax.ShapeDtypeStruct((2, 2 * HD,...  25 us
  transfers between devices with their start and end apart: 1, of which 0 were waited for; matrix products, arithmetic and copies ran while one was open for 1% of the time, Pallas kernels for 20%

profile of v6, /device:TPU:1, one launch (start us, length us, event | category | flops | bytes accessed | tf_op | source)
XLA Modules:
  0.0 320.1 jit_solution(11573793541532869886)
XLA Ops:
  0.6 144.2 %pack.1 = bf16[4,576,1024]{2,1,0:T(8,128)(2,1)} custom-call(bf16[4608,512]{1,0:T(8,128)(2,1)} %wq.3, bf16[4608,256]{1,0:T(8,128)(2,1)} %wk.3, bf16[4608,256]{1,0:T(8,128)(2,1)} %wv.3), custom_call_target="tpu_custom_call" | custom-call | tf_op jit(solution)/shard_map/pack/pallas_call | solution.py:87
  144.8 5.9 %all-to-all-start = ((bf16[4,576,1024]{2,1,0:T(8,128)(2,1)}), bf16[4,576,1024]{2,1,0:T(8,128)(2,1)}, u32[]{:S(2)}, u32[]{:S(2)}) async-start(bf16[4,576,1024]{2,1,0:T(8,128)(2,1)} %pack.1), calls=%async_computation | async-start | bytes 9437184 | tf_op jit(solution)/shard_map/all_to_all | solution.py:845
  150.7 39.9 %gather.1 = (bf16[2,2,512,256]{3,2,1,0:T(8,128)(2,1)}, bf16[10,2,512,128]{3,2,1,0:T(8,128)(2,1)}, bf16[2,4608,512]{2,1,0:T(8,128)(2,1)}) custom-call(bf16[512,512]{1,0:T(8,128)(2,1)} %q.1, bf16[512,512]{1,0:T(8,128)(2,1)} %g.1, bf16[512,256]{1,0:T(8,128)(2,1)} %k.1, bf16[512,256]{1,0:T(8,128)(2,1)} %v.1, bf16[512,4608]{1,0:T(8,128)(2,1)} %n_hbm.1), custom_call_target="tpu_custom_call" | custom-call | tf_op jit(solution)/shard_map/gather/pallas_call | solution.py:219
  190.6 1.8 multiply_sine_fusion
  192.5 25.0 %attend.1 = (bf16[2,256,512]{2,1,0:T(8,128)(2,1)}, bf16[8,2,512,128]{3,2,1,0:T(8,128)(2,1)}, f32[2,2,512,128]{3,2,1,0:T(8,128)}) custom-call(s32[16]{0:T(128)} %valid.1, s32[1]{0:T(128)} %bitcast.base, bf16[2,2,512,256]{3,2,1,0:T(8,128)(2,1)} %get-tuple-element.16.qg, bf16[10,2,4,128,128]{4,3,2,1,0:T(8,128)(2,1)} %bitcast.3, ...), custom_call_target="tpu_custom_call" | custom-call | flops 25999998976 | bytes 8388608 | tf_op jit(solution)/shard_map/attend/pallas_call | solution.py:442
  217.4 0.0 all-to-all-done.w_rows
  217.5 100.4 %finish.1 = (bf16[576,512]{1,0:T(8,128)(2,1)}, bf16[2,2,288,256]{3,2,1,0:T(8,128)(2,1)}) custom-call(bf16[2,256,512]{2,1,0:T(8,128)(2,1)} %get-tuple-element.18.dq, bf16[8,2,512,128]{3,2,1,0:T(8,128)(2,1)} %get-tuple-element.19.dkv, f32[2,2,512,128]{3,2,1,0:T(8,128)} %get-tuple-element.20.own_hbm, bf16[2,4608,512]{2,1,0:T(8,128)(2,1)} %get-tuple-element.21.turned_hbm, ...), custom_call_target="tpu_custom_call" | custom-call | tf_op jit(solution)/shard_map/finish/pallas_call | solution.py:775
  317.9 2.3 emit.1
  (2 shorter events, 0.0 us)
Async XLA Ops:
  144.8 72.6 %all-to-all-start = ((bf16[4,576,1024]{2,1,0:T(8,128)(2,1)}), bf16[4,576,1024]{2,1,0:T(8,128)(2,1)}, u32[]{:S(2)}, u32[]{:S(2)}) async-start(bf16[4,576,1024]{2,1,0:T(8,128)(2,1)} %pack.1), calls=%async_computation | async-start | bytes 9437184 | tf_op jit(solution)/shard_map/all_to_all | solution.py:845
